TPU v7x, 512 devices: a whole 4x4x16 slice. The times are simulated.
512 devices in a mesh: op: 4 (over x), sec: 128 (over z, y, core).
Axes of the slice: x: 4, y: 4, z: 16, core: 2. Of those that a mesh axis runs over, the one named last changes fastest.
Arguments:
- wave: bfloat16 [8192, 8192], P(None, 'sec'), may hold values from -6 to 6
- left_env: bfloat16 [4, 128, 64, 64], P('op', 'sec'), may hold values from -1 to 1
- right_env: bfloat16 [4, 128, 64, 64], P('op', 'sec'), may hold values from -0.5 to 0.5
- left_map: int32 [4, 128], P('op'), may hold values from 0 to 127
- right_map: int32 [4, 128], P('op'), may hold values from 0 to 127
- left_dims: int32 [128], replicated, may hold values from 1 to 64, 6144 in all
- right_dims: int32 [128], replicated, may hold values from 1 to 64, 6144 in all
Outputs:
- product: bfloat16 [8192, 8192], P('sec')
Inputs may be any that keep to these rules, and one draw needn't show every extreme that they name: `left_dims`: the sizes sum to 6144 and the largest is exactly 64. `right_dims`: the sizes sum to 6144 and the largest is exactly 64.
All inputs are finite; a program needn't handle non-finite values.
Results may differ from a plain program's by a relative error of at most 0.023.
Values may be sent and summed in bfloat16 or wider, within the bound.
No kernel may reach another device: no remote copies, remote signals or barrier semaphores. Data moves between devices by JAX's collectives and lax.ppermute only.
A program may use at most 64 MiB of HBM per device.

v0:
```python
import jax
import jax.numpy as jnp
from jax import lax
from jax.sharding import PartitionSpec as P


def state_mask(extents, states):
    levels = jnp.arange(states, dtype=jnp.int32)
    return (levels[None, :] < extents[:, None]).astype(jnp.float32).reshape(-1)


def left_terms(matrix, left_full, left_map):
    sectors, states = (left_full.shape[1], left_full.shape[2])
    blocks = matrix.reshape(sectors, states, -1)[left_map]
    return jnp.einsum("waik,wakn->wain", left_full, blocks, preferred_element_type=jnp.float32)


def right_terms(matrix, right_full, right_map):
    sectors, states = (right_full.shape[1], right_full.shape[2])
    blocks = matrix.reshape(matrix.shape[0], sectors, states)[:, right_map, :]
    result = jnp.einsum("mwbk,wbkj->wmbj", blocks, right_full, preferred_element_type=jnp.float32)
    return result.reshape(right_full.shape[0], matrix.shape[0], sectors * states)


def on_device(wave, left_env, right_env, left_map, right_map, left_dims, right_dims):
    left_full, right_full = (
        lax.all_gather(left_env, "sec", axis=1, tiled=True),
        lax.all_gather(right_env, "sec", axis=1, tiled=True),
    )
    term_count, sectors, states = (left_full.shape[0], left_full.shape[1], left_full.shape[2])
    columns = wave.shape[1]
    sector_index = lax.axis_index("sec")
    row_all = state_mask(left_dims, states)
    col_all = state_mask(right_dims, states)
    col_mine = lax.dynamic_slice_in_dim(col_all, sector_index * columns, columns)
    row_mine = lax.dynamic_slice_in_dim(row_all, sector_index * columns, columns)
    initial = jnp.where(row_all[:, None] * col_mine[None, :] > 0, wave, jnp.zeros_like(wave))

    def to_rows(middle):
        arrived = lax.all_to_all(middle, "sec", split_axis=1, concat_axis=3, tiled=True)
        arrived = arrived.reshape(term_count, -1, sectors, states)
        picked = jax.vmap(lambda portion, source: portion[:, source, :])(arrived, right_map)
        summed = jnp.einsum(
            "wmbk,wbkj->mbj", picked, right_full, preferred_element_type=jnp.float32
        )
        return summed.reshape(arrived.shape[1], sectors * states)

    middle_one = left_terms(initial, left_full, left_map).astype(jnp.bfloat16)
    partial_one = to_rows(middle_one)
    row_layout_mask = row_mine[:, None] * col_all[None, :]
    summed_one = lax.psum(partial_one.astype(jnp.bfloat16), "op").astype(jnp.float32)
    first_pass = (summed_one * row_layout_mask).astype(jnp.bfloat16)
    middle_two = right_terms(first_pass, right_full, right_map).astype(jnp.bfloat16)
    arrived_two = lax.all_to_all(middle_two, "sec", split_axis=2, concat_axis=1, tiled=True)
    arrived_two = arrived_two.reshape(term_count, sectors, states, columns)
    picked_two = jax.vmap(lambda portion, source: portion[source])(arrived_two, left_map)
    partial_two = jnp.einsum(
        "waik,wakn->ain", left_full, picked_two, preferred_element_type=jnp.float32
    )
    partial_two = partial_two.reshape(sectors * states, columns)
    col_layout_mask = row_all[:, None] * col_mine[None, :]
    summed_two = lax.psum(partial_two.astype(jnp.bfloat16), "op").astype(jnp.float32)
    second_pass = (summed_two * col_layout_mask).astype(jnp.bfloat16)
    middle_three = left_terms(second_pass, left_full, left_map).astype(jnp.bfloat16)
    partial_three = to_rows(middle_three)
    summed_three = lax.psum(partial_three.astype(jnp.bfloat16), "op").astype(jnp.float32)
    return (summed_three * row_layout_mask).astype(jnp.bfloat16)


def solution(mesh):
    placed = (
        P(None, "sec"),
        P("op", "sec", None, None),
        P("op", "sec", None, None),
        P("op", None),
        P("op", None),
        P(),
        P(),
    )
    return jax.shard_map(
        on_device, mesh=mesh, in_specs=placed, out_specs=P("sec", None), check_vma=False
    )
```

profile of v0, /device:TPU:1, one launch (start us, length us, event | category | flops | bytes accessed | tf_op | source)
XLA Modules:
  0.0 771.0 jit_solution(1594326559872510326)
XLA Ops:
  14.9 142.0 %all-gather.3.cloned.1.call-done = bf16[1,128,64,64]{3,2,0,1:T(8,128)(2,1)} async-done(((bf16[1,1,64,64]{3,2,0,1:T(8,128)(2,1)}), bf16[1,128,64,64]{3,2,0,1:T(8,128)(2,1)}) %all-gather.3.cloned.1.call-update) | async-done | bytes 1048592 | tf_op jit(solution)/shard_map/all_gather | solution.py:27
  157.0 4.2 fusion.43
  161.2 4.7 reshape.191
  165.8 11.2 %all-to-all-start = ((bf16[128,2,2048]{2,1,0:T(2,128)(2,1)}), bf16[128,2,2048]{2,1,0:T(2,128)(2,1)S(1)}, u32[]{:S(2)}, u32[]{:S(2)}) async-start(bf16[128,2,2048]{2,1,0:T(2,128)(2,1)} %reshape.191), calls=%async_computation | async-start | bytes 2097152 | tf_op jit(solution)/shard_map/all_to_all | solution.py:40
  178.1 51.5 %all-to-all-done = bf16[128,2,2048]{2,1,0:T(2,128)(2,1)S(1)} async-done(((bf16[128,2,2048]{2,1,0:T(2,128)(2,1)}), bf16[128,2,2048]{2,1,0:T(2,128)(2,1)S(1)}, u32[]{:S(2)}, u32[]{:S(2)}) %all-to-all-start) | async-done | bytes 1048608 | tf_op jit(solution)/shard_map/all_to_all | solution.py:40
  235.1 88.8 %all-gather.5.cloned.1.call-done = bf16[1,128,64,64]{3,2,0,1:T(8,128)(2,1)} async-done(((bf16[1,1,64,64]{3,2,0,1:T(8,128)(2,1)}), bf16[1,128,64,64]{3,2,0,1:T(8,128)(2,1)}) %all-gather.5.cloned.1.call-update) | async-done | bytes 1048592 | tf_op jit(solution)/shard_map/all_gather | solution.py:28
  330.4 55.6 %all-reduce.4.cloned.1.call-done = bf16[64,8192]{1,0:T(8,128)(2,1)} async-done(((bf16[64,8192]{1,0:T(8,128)(2,1)}), bf16[64,8192]{1,0:T(8,128)(2,1)}) %all-reduce.4.cloned.1.call-update) | async-done | bytes 1048592 | tf_op jit(solution)/shard_map/psum | solution.py:51
  392.4 3.9 gather_fusion.1
  396.3 3.6 convert_bitcast_fusion.3
  400.0 3.2 copy.48
  403.2 6.2 reshape.189
  409.9 45.7 %reduce = bf16[8192,64]{1,0:T(8,128)(2,1)S(1)} reduce(bf16[8192,1,64]{2,1,0:T(2,128)(2,1)} %bitcast.127, bf16[]{:T(256)} %broadcast.99), dimensions={1}, to_apply=%bitcast.105.reduce_sub_computation | reduce | bytes 2097154
  458.0 18.5 %all-to-all-start.1 = ((bf16[128,2,2048]{2,1,0:T(2,128)(2,1)}), bf16[128,2,2048]{2,1,0:T(2,128)(2,1)S(1)}, u32[]{:S(2)}, u32[]{:S(2)}) async-start(bf16[128,2,2048]{2,1,0:T(2,128)(2,1)} %reshape.193), calls=%async_computation.1 | async-start | bytes 2097152 | tf_op jit(solution)/shard_map/all_to_all | solution.py:54
  476.6 52.0 %all-to-all-done.1 = bf16[128,2,2048]{2,1,0:T(2,128)(2,1)S(1)} async-done(((bf16[128,2,2048]{2,1,0:T(2,128)(2,1)}), bf16[128,2,2048]{2,1,0:T(2,128)(2,1)S(1)}, u32[]{:S(2)}, u32[]{:S(2)}) %all-to-all-start.1) | async-done | bytes 1048608 | tf_op jit(solution)/shard_map/all_to_all | solution.py:54
  528.6 7.2 reshape.194
  541.0 3.9 gather_fusion.4
  550.5 4.1 convert_element_type.127
  554.7 54.1 %all-reduce.6.cloned.1.call-done = bf16[8192,64]{0,1:T(8,128)(2,1)} async-done(((bf16[8192,64]{0,1:T(8,128)(2,1)}), bf16[8192,64]{0,1:T(8,128)(2,1)}) %all-reduce.6.cloned.1.call-update) | async-done | bytes 1048592 | tf_op jit(solution)/shard_map/psum | solution.py:62
  612.1 3.7 gather_fusion.2
  615.9 4.2 fusion.46
  620.1 3.9 reshape.195
  624.0 70.6 %all_to_all.45 = bf16[128,2,2048]{2,1,0:T(2,128)(2,1)S(1)} all-to-all(bf16[128,2,2048]{2,1,0:T(2,128)(2,1)S(1)} %reshape.195), channel_id=1, replica_groups=mesh['op'=4,'sec'=128] {'sec'}, dimensions={0} | all-to-all | bytes 2097152 | tf_op jit(solution)/shard_map/all_to_all | solution.py:40
  697.4 3.9 gather_fusion.5
  707.7 54.1 %all-reduce.8.cloned.1.call-done = bf16[64,8192]{1,0:T(8,128)(2,1)} async-done(((bf16[64,8192]{1,0:T(8,128)(2,1)}), bf16[64,8192]{1,0:T(8,128)(2,1)}) %all-reduce.8.cloned.1.call-update) | async-done | bytes 1048592 | tf_op jit(solution)/shard_map/psum | solution.py:66
  (60 shorter events, 56.5 us)
Async XLA Ops:
  6.5 150.4 %all-gather.3.cloned.1.call-start = ((), (), s32[]{:S(2)}) async-start(), calls=%async_computation.3 | async-start | bytes 2113536 | tf_op jit(solution)/shard_map/all_gather | solution.py:27
  10.6 1.8 copy-start.3
  161.2 16.9 %copy-start.4 = (s32[1,128]{1,0:T(1,128)S(1)}, s32[1,128]{1,0:T(1,128)}, u32[]{:S(2)}) copy-start(s32[1,128]{1,0:T(1,128)} %param.11) | copy-start | bytes 1540
  165.8 63.9 %all-to-all-start = ((bf16[128,2,2048]{2,1,0:T(2,128)(2,1)}), bf16[128,2,2048]{2,1,0:T(2,128)(2,1)S(1)}, u32[]{:S(2)}, u32[]{:S(2)}) async-start(bf16[128,2,2048]{2,1,0:T(2,128)(2,1)} %reshape.191), calls=%async_computation | async-start | bytes 2097152 | tf_op jit(solution)/shard_map/all_to_all | solution.py:40
  177.0 146.9 %all-gather.5.cloned.1.call-start = ((), (), s32[]{:S(2)}) async-start(), calls=%async_computation.4 | async-start | bytes 2113536 | tf_op jit(solution)/shard_map/all_gather | solution.py:28
  177.8 208.2 %all-reduce.4.cloned.1.call-start = ((), (), s32[]{:S(2)}) async-start(), calls=%async_computation.5 | async-start | bytes 2097152 | tf_op jit(solution)/shard_map/psum | solution.py:51
  392.4 3.9 copy-start.1
  458.0 70.6 %all-to-all-start.1 = ((bf16[128,2,2048]{2,1,0:T(2,128)(2,1)}), bf16[128,2,2048]{2,1,0:T(2,128)(2,1)S(1)}, u32[]{:S(2)}, u32[]{:S(2)}) async-start(bf16[128,2,2048]{2,1,0:T(2,128)(2,1)} %reshape.193), calls=%async_computation.1 | async-start | bytes 2097152 | tf_op jit(solution)/shard_map/all_to_all | solution.py:54
  476.5 132.3 %all-reduce.6.cloned.1.call-start = ((), (), s32[]{:S(2)}) async-start(), calls=%async_computation.6 | async-start | bytes 2097152 | tf_op jit(solution)/shard_map/psum | solution.py:62
  541.0 3.9 copy-start
  554.7 207.1 %all-reduce.8.cloned.1.call-start = ((), (), s32[]{:S(2)}) async-start(), calls=%async_computation.7 | async-start | bytes 2097152 | tf_op jit(solution)/shard_map/psum | solution.py:66
  697.4 3.9 copy-start.2
Sparse Core Ops, SparseCore 0:
  10.5 146.4 all-gather.2
  181.0 142.9 all-gather.4
  330.4 55.4 all-reduce.3
  554.8 53.9 all-reduce.5
  707.8 53.9 all-reduce.7
where the time goes:
time: 777 us; the launch traced here: 771 us
  waiting for transfers between devices  500 us (64%)
  local copies, waits for them, and re-layouts  83 us (11%)
  blocking collectives  70.6 us (9%)
  other arithmetic  54.4 us (7%)
  starting transfers between devices  30.1 us (4%)
  matrix products  19.7 us (3%)
  between operations  13.6 us (2%)
    all_gather x1, waiting for transfers between devices, on_device(): lax.all_gather(left_env, 'sec', axis=1, tiled=True)  142 us
    all_gather x1, waiting for transfers between devices, on_device(): lax.all_gather(right_env, 'sec', axis=1, tiled=True)  88.8 us
    all_to_all x1, blocking collectives, to_rows(): lax.all_to_all(middle, 'sec', split_axis=1, concat_axis=3, tiled=True)  70.6 us
    psum x1, waiting for transfers between devices, on_device(): lax.psum(partial_one.astype(jnp.bfloat16), 'op').astype(jnp.float32)  55.6 us
    psum x1, waiting for transfers between devices, on_device(): lax.psum(partial_two.astype(jnp.bfloat16), 'op').astype(jnp.float32)  54.1 us
    psum x1, waiting for transfers between devices, on_device(): lax.psum(partial_three.astype(jnp.bfloat16), 'op').astype(jnp.float32)  54.1 us
    all_to_all x1, waiting for transfers between devices, on_device(): lax.all_to_all(middle_two, 'sec', split_axis=2, concat_axis=1, tiled=True)  52 us
    all_to_all x1, waiting for transfers between devices, to_rows(): lax.all_to_all(middle, 'sec', split_axis=1, concat_axis=3, tiled=True)  51.5 us
  transfers between devices with their start and end apart: 7, of which 7 were waited for; matrix products, arithmetic and copies ran while one was open for 2% of the time, Pallas kernels for 0%

commit v1 on v0

v1 whole, which is shorter than its diff:
```python
import functools

import jax
import jax.numpy as jnp
from jax import lax
from jax.experimental import pallas as pl
from jax.experimental.pallas import tpu as pltpu
from jax.sharding import Mesh
from jax.sharding import PartitionSpec as P

BF16, F32 = jnp.bfloat16, jnp.float32
NT = (((1,), (1,)), ((), ()))
SEC = ("z", "y", "c")
ALL = ("op",) + SEC


def iota(shape, axis):
    return lax.broadcasted_iota(jnp.int32, shape, axis)


def spot(info, sizes, sector):
    nz, ny = sizes
    core, rest = sector & 1, sector >> 1
    return ((core ^ info[2]) * ny + lax.rem(rest, ny)) * nz + lax.div(rest, ny)


def fold_out(out_ref, pair, count, first, second):
    for q in range(4):
        rows = jnp.concatenate([first[8 * q : 8 * q + 8], second[8 * q : 8 * q + 8]], axis=0)
        start = pl.multiple_of(q * count * 8 + pair * 16, 16)
        out_ref[pl.ds(start, 16), :] = rows.astype(BF16)


def left_kernel(count, sizes, info, source, row_dims, col_dims, wave, env, out, blocks):
    lane = iota((64, 128), 1)
    low = lane < 64
    alive = iota((64, 128), 0) < col_dims[info[1]]

    def spread(pair, carry):
        value = wave[:, pl.ds(pl.multiple_of(pair * 128, 128), 128)].astype(F32)
        extent = jnp.where(low, row_dims[2 * pair], row_dims[2 * pair + 1] + 64)
        value = jnp.where(alive & (lane < extent), value, 0.0)
        turned = pltpu.roll(value, 64, 1)
        blocks[2 * pair] = jnp.where(low, value, turned).astype(BF16)
        blocks[2 * pair + 1] = jnp.where(low, turned, value).astype(BF16)
        return carry

    lax.fori_loop(0, count // 2, spread, 0, unroll=2)
    zero = jnp.zeros((64, 128), BF16)

    def product(block):
        place = spot(info, sizes, block)
        e = env[pl.ds(pl.multiple_of(place * 32, 32), 32), :]
        f = blocks[source[block]]
        rhs = jnp.concatenate([jnp.where(low, f, zero), jnp.where(low, zero, f)], axis=0)
        return lax.dot_general(e, rhs, NT, preferred_element_type=F32)

    def step(pair, carry):
        fold_out(out, pair, count, product(2 * pair), product(2 * pair + 1))
        return carry

    lax.fori_loop(0, count // 2, step, 0, unroll=2)


def middle_kernel(
    count, sizes, turn, last, info, source, row_dims, col_dims,
    arrived, env_0, env_1, env_2, env_3, out, env, tiles, held, sems,
):
    copies = [
        pltpu.make_async_copy(ref, env.at[info[3 + i]], sems.at[i])
        for i, ref in enumerate((env_0, env_1, env_2, env_3))
    ]
    for copy in copies:
        copy.start()
    lane8 = iota((16, 128), 1)
    low8 = lane8 < 64
    bit0, bit1 = (lane8 & 8) == 0, (lane8 & 16) == 0

    def place(pair, carry):
        got = [
            arrived[pl.ds(pl.multiple_of(w * count * 8 + pair * 16, 16), 16), :].astype(F32)
            for w in range(4)
        ]
        if turn:
            for a, b in ((0, 1), (2, 3)):
                one, two = got[a], got[b]
                got[a] = jnp.where(bit0, one, pltpu.roll(two, 8, 1))
                got[b] = jnp.where(bit0, pltpu.roll(one, 120, 1), two)
            for a, b in ((0, 2), (1, 3)):
                one, two = got[a], got[b]
                got[a] = jnp.where(bit1, one, pltpu.roll(two, 16, 1))
                got[b] = jnp.where(bit1, pltpu.roll(one, 112, 1), two)
        for w in range(4):
            turned = pltpu.roll(got[w], 64, 1)
            top, bottom = jnp.where(low8, got[w], turned), jnp.where(low8, turned, got[w])
            for k in range(2):
                rows = slice(8 * k, 8 * k + 8)
                tile = jnp.concatenate([top[rows], bottom[rows]], axis=0)
                tiles[w, 2 * pair + k] = tile.astype(BF16)
        return carry

    lax.fori_loop(0, count // 2, place, 0, unroll=2)
    for copy in copies:
        copy.wait()

    low = iota((16, 128), 1) < 64
    upper = iota((16, 128), 0) < 8
    zero = jnp.zeros((16, 128), BF16)
    pad = jnp.zeros((32, 96), F32)
    row = iota((16, 128), 0)
    natural = (row & 7) + (row >> 3) * 32 + info[0] * 8
    row_alive = natural < row_dims[info[1]]
    lane_in = iota((16, 128), 1) & 63

    def env_of(block):
        start = pl.multiple_of(spot(info, sizes, block) * 32, 32)
        return jnp.concatenate([env[w, pl.ds(start, 32), :] for w in range(4)], axis=1)

    def summed(block):
        lhs = []
        for w in range(4):
            t = tiles[w, source[w, block]]
            lhs.append(jnp.concatenate([jnp.where(low, t, zero), jnp.where(low, zero, t)], axis=0))
        lhs = jnp.concatenate(lhs, axis=1)
        total = lax.dot_general(lhs, env_of(block), NT, preferred_element_type=F32)
        total = jnp.concatenate([total, pad], axis=1)
        total = total[:16] + pltpu.roll(total[16:], 32, 1)
        return jnp.where(row_alive & (lane_in < col_dims[block]), total, 0.0)

    if last:

        def finish(pair, carry):
            value = summed(2 * pair) + pltpu.roll(summed(2 * pair + 1), 64, 1)
            out[:, pl.ds(pl.multiple_of(pair * 128, 128), 128)] = value.astype(BF16)
            return carry

        lax.fori_loop(0, count // 2, finish, 0, unroll=2)
        return

    def keep(block, carry):
        value = summed(block)
        value = value + pltpu.roll(value, 64, 1)
        first, second = value[:8], value[8:]
        held[block] = jnp.concatenate([first, first, second, second], axis=0).astype(BF16)
        return carry

    lax.fori_loop(0, count, keep, 0, unroll=4)
    masks = [[(upper if p == 0 else ~upper) & (low if h == 0 else ~low) for h in range(2)] for p in range(2)]

    def product(block):
        slots = []
        for w in range(4):
            both = held[source[w, block]]
            rows = []
            for h in range(2):
                for half in range(2):
                    tile = jnp.where(masks[w & 1][h], both[16 * half : 16 * half + 16], zero)
                    rows += [tile, zero] if w < 2 else [zero, tile]
            slots.append(jnp.concatenate(rows, axis=0))
        rhs = jnp.concatenate(slots, axis=1)
        return lax.dot_general(env_of(block), rhs, NT, preferred_element_type=F32)

    def step(pair, carry):
        fold_out(out, pair, count, product(2 * pair), product(2 * pair + 1))
        return carry

    lax.fori_loop(0, count // 2, step, 0, unroll=2)


SMEM = pl.BlockSpec(memory_space=pltpu.SMEM)
VMEM = pl.BlockSpec(memory_space=pltpu.VMEM)
ANY = pl.BlockSpec(memory_space=pl.ANY)


def left_stage(count, sizes, info, source, row_dims, col_dims, wave, env):
    return pl.pallas_call(
        functools.partial(left_kernel, count, sizes),
        out_shape=jax.ShapeDtypeStruct((count * 32, 128), BF16),
        in_specs=[SMEM] * 4 + [VMEM] * 2,
        out_specs=VMEM,
        scratch_shapes=[pltpu.VMEM((count, 64, 128), BF16)],
        cost_estimate=pl.CostEstimate(flops=count * 2**20, bytes_accessed=count * 24576, transcendentals=0),
        name="left_stage",
    )(info, source, row_dims, col_dims, wave, env)


def middle_stage(count, sizes, turn, last, info, source, row_dims, col_dims, arrived, envs):
    shape = (16, count * 64) if last else (count * 32, 128)
    return pl.pallas_call(
        functools.partial(middle_kernel, count, sizes, turn, last),
        out_shape=jax.ShapeDtypeStruct(shape, BF16),
        in_specs=[SMEM] * 4 + [VMEM] + [ANY] * 4,
        out_specs=VMEM,
        scratch_shapes=[
            pltpu.VMEM((4, count * 32, 128), BF16),
            pltpu.VMEM((4, count, 16, 128), BF16),
            pltpu.VMEM((count, 32, 128), BF16),
            pltpu.SemaphoreType.DMA((4,)),
        ],
        cost_estimate=pl.CostEstimate(flops=count * 2**23, bytes_accessed=count * 49152, transcendentals=0),
        name="last_stage" if last else "middle_stage",
    )(info, source, row_dims, col_dims, arrived, *envs)


def fold(block):
    return jnp.concatenate([block[:32], block[32:]], axis=1)


def copies_to(value, axis, size):
    return lax.all_to_all(jnp.broadcast_to(value, (size,) + value.shape), axis, 0, 0, tiled=True)


def exchange(chunks, devices):
    shape = chunks.shape
    return lax.all_to_all(chunks.reshape(devices, 8, 128), ALL, 0, 0, tiled=True).reshape(shape)


def on_device(sizes, wave, left_env, right_env, left_map, right_map, left_dims, right_dims):
    nz, ny = sizes
    count = left_map.shape[1]
    me, core = lax.axis_index("op"), lax.axis_index("c")
    sector = lax.axis_index(SEC)
    shifts = (0, 1, 3, 2)
    info = jnp.stack([me, sector, core] + [lax.rem(me + 4 - s, 4) for s in shifts] + [me]).astype(jnp.int32)

    maps = copies_to(jnp.stack([left_map[0], right_map[0]]), "op", 4)
    own = jnp.stack([fold(left_env[0, 0]), fold(right_env[0, 0].T)])
    over_z = copies_to(own, "z", nz)
    over_y = copies_to(over_z, "y", ny)
    other = lax.ppermute(over_y, "c", [(0, 1), (1, 0)])

    def gathered(which):
        both = jnp.stack([over_y[:, :, which], other[:, :, which]])
        return both.reshape(count * 32, 128)

    left_own, right_own = gathered(0), gathered(1)

    def over_op(value):
        moved = [lax.ppermute(value, "op", [(i, (i + s) % 4) for i in range(4)]) for s in shifts[1:]]
        return [value] + moved

    chunks = left_stage(count, sizes, info, left_map[0], left_dims, right_dims, wave.T, left_own)
    rights = over_op(right_own)
    arrived = exchange(chunks, 4 * count)
    left_late, arrived = lax.optimization_barrier((left_own, arrived))
    chunks = middle_stage(
        count, sizes, False, False, info, maps[:, 1], left_dims, right_dims, arrived, rights
    )
    lefts = over_op(left_late)
    arrived = exchange(chunks, 4 * count)
    chunks = middle_stage(
        count, sizes, True, False, info, maps[:, 0], right_dims, left_dims, arrived, lefts
    )
    arrived = exchange(chunks, 4 * count)
    piece = middle_stage(
        count, sizes, True, True, info, maps[:, 1], left_dims, right_dims, arrived, rights
    )
    pieces = copies_to(piece, "op", 4)
    return pieces.reshape(4, 2, 8, count * 64).swapaxes(0, 1).reshape(64, count * 64)


def solution(mesh):
    n_op, n_sec = mesh.devices.shape
    ny = 4
    nz = n_sec // (2 * ny)
    split = Mesh(mesh.devices.reshape(n_op, nz, ny, 2), ALL)
    placed = (
        P(None, SEC),
        P("op", SEC, None, None),
        P("op", SEC, None, None),
        P("op", None),
        P("op", None),
        P(),
        P(),
    )
    return jax.shard_map(
        functools.partial(on_device, (nz, ny)),
        mesh=split, in_specs=placed, out_specs=P(SEC, None), check_vma=False,
    )
```

time: 777 us -> 405 us (0.52)
  waiting for transfers between devices: 500 us -> 101 us
  Pallas kernels: 0 us -> 82.5 us
  local copies, waits for them, and re-layouts: 83 us -> 7.97 us
  blocking collectives: 70.6 us -> 140 us
  other arithmetic: 54.4 us -> 1.26 us
  starting transfers between devices: 30.1 us -> 70.3 us
  matrix products: 19.7 us -> 0 us
  between operations: 13.6 us -> 0.25 us
    all_gather x2 -> x0, waiting for transfers between devices: 231 us -> none  [the longest x1 142 us: on_device(): lax.all_gather(left_env, 'sec', axis=1, tiled=True)]
    psum x3 -> x0, waiting for transfers between devices: 164 us -> none  [the longest x1 55.6 us: on_device(): lax.psum(partial_one.astype(jnp.bfloat16), 'op').astype(jnp.float32)]
    pallas_call x0 -> x4, Pallas kernels: none -> 82.5 us  [the longest x3 71.2 us: middle_stage(): pl.pallas_call(functools.partial(middle_kernel, count, sizes, turn, last)...]
    all_to_all x1 -> x4, blocking collectives: 70.6 us -> 140 us  [the longest x1 79.7 us: exchange(): lax.all_to_all(chunks.reshape(devices, 8, 128), ALL, 0, 0, tiled=True)]
    all_to_all x2 -> x3, waiting for transfers between devices: 104 us -> 46.8 us  [the longest x2 46.8 us: exchange(): lax.all_to_all(chunks.reshape(devices, 8, 128), ALL, 0, 0, tiled=True)]
    ppermute x0 -> x7, waiting for transfers between devices: none -> 54.1 us  [the longest x6 54.1 us: over_op(): lax.ppermute(value, 'op', [(i, (i + s) % 4) for i in range(4)])]
    unnamed x1 -> x0, other arithmetic: 45.7 us -> none
    ppermute x0 -> x7, starting transfers between devices: none -> 29 us  [the longest x6 20.1 us: over_op(): lax.ppermute(value, 'op', [(i, (i + s) % 4) for i in range(4)])]
  transfers between devices with their start and end apart: 7 -> 10, of which waited for: 7 -> 5; matrix products, arithmetic and copies ran while one was open for 2% -> 1% of each run, Pallas kernels for 0% -> 3%
where the time goes in v1:
time: 405 us; the launch traced here: 404 us
  blocking collectives  140 us (35%)
  waiting for transfers between devices  101 us (25%)
  Pallas kernels  82.5 us (20%)
  starting transfers between devices  70.3 us (17%)
  local copies, waits for them, and re-layouts  7.97 us (2%)
    all_to_all x1, blocking collectives, exchange(): lax.all_to_all(chunks.reshape(devices, 8, 128), ALL, 0, 0, tiled=True)  79.7 us
    pallas_call x3, Pallas kernels, middle_stage(): pl.pallas_call(functools.partial(middle_kernel, count, sizes, turn, last)...  71.2 us
    all_to_all x3, blocking collectives, copies_to(): lax.all_to_all(jnp.broadcast_to(value, (size,) + value.shape), axis, 0, 0...  60.8 us
    ppermute x6, waiting for transfers between devices, over_op(): lax.ppermute(value, 'op', [(i, (i + s) % 4) for i in range(4)])  54.1 us
    all_to_all x2, waiting for transfers between devices, exchange(): lax.all_to_all(chunks.reshape(devices, 8, 128), ALL, 0, 0, tiled=True)  46.8 us
    all_to_all x2, starting transfers between devices, exchange(): lax.all_to_all(chunks.reshape(devices, 8, 128), ALL, 0, 0, tiled=True)  37.3 us
    ppermute x6, starting transfers between devices, over_op(): lax.ppermute(value, 'op', [(i, (i + s) % 4) for i in range(4)])  20.1 us
    pallas_call x1, Pallas kernels, left_stage(): pl.pallas_call(functools.partial(left_kernel, count, sizes), out_shape=ja...  11.3 us
  transfers between devices with their start and end apart: 10, of which 5 were waited for; matrix products, arithmetic and copies ran while one was open for 1% of the time, Pallas kernels for 3%

profile of v1, /device:TPU:1, one launch (start us, length us, event | category | flops | bytes accessed | tf_op | source)
XLA Modules:
  0.0 403.7 jit_solution(9873965635853720003)
XLA Ops:
  1.7 29.3 %all_to_all.35 = bf16[16,2,32,128]{3,2,1,0:T(8,128)(2,1)S(1)} all-to-all(bf16[16,2,32,128]{3,2,1,0:T(8,128)(2,1)S(1)} %broadcast_in_dim.13), channel_id=1, replica_groups=mesh['op'=4,'z'=16,'y'=4,'c'=2] {'z'}, dimensions={0} | all-to-all | bytes 524288 | tf_op jit(solution)/shard_map/all_to_all | solution.py:210
  31.2 13.7 %all_to_all.36 = bf16[4,16,2,32,128]{4,3,1,2,0:T(8,128)(2,1)S(1)} all-to-all(bf16[4,16,2,32,128]{4,3,1,2,0:T(8,128)(2,1)S(1)} %broadcast_in_dim.14), channel_id=1, replica_groups=mesh['op'=4,'z'=16,'y'=4,'c'=2] {'y'}, dimensions={0} | all-to-all | bytes 2097152 | tf_op jit(solution)/shard_map/all_to_all | solution.py:210
  45.0 8.9 %collective-permute-start = (bf16[4,16,2,32,128]{4,3,1,0,2:T(8,128)(2,1)S(1)}, bf16[4,16,2,32,128]{4,3,1,0,2:T(8,128)(2,1)S(1)}, u32[]{:S(2)}, u32[]{:S(2)}) collective-permute-start(bf16[4,16,2,32,128]{4,3,1,0,2:T(8,128)(2,1)S(1)} %copy.22), channel_id=1, source_target_pairs={{0,1},{1,0},{2,3},{3,2},{4,5},{5,4},{6,7},{7,6},{8,9},{9,8},{10,11... | collective-permute-start | bytes 3145736 | tf_op jit(solution)/shard_map/ppermute | solution.py:230
  54.6 4.0 all-to-all-start
  60.4 11.3 %left_stage.1 = bf16[4096,128]{1,0:T(8,128)(2,1)} custom-call(s32[8]{0:T(128)} %stack.50.info, s32[128]{0:T(128)} %bitcast.68, s32[128]{0:T(128)} %row_dims.7, s32[128]{0:T(128)} %col_dims.7, bf16[64,8192]{1,0:T(8,128)(2,1)} %bitcast.63, bf16[4096,128]{1,0:T(8,128)(2,1)} %bitcast.46), custom_call_target="tpu_custom_call" | custom-call | flops 134217728 | bytes 3145728 | tf_op jit(solution)/shard_map/left_stage/pallas_call | solution.py:176
  71.7 16.3 %all-to-all-start.3 = ((bf16[512,8,128]{2,1,0:T(8,128)(2,1)}), bf16[512,8,128]{2,1,0:T(8,128)(2,1)S(1)}, u32[]{:S(2)}, u32[]{:S(2)}) async-start(bf16[512,8,128]{2,1,0:T(8,128)(2,1)} %bitcast.61), calls=%async_computation.3 | async-start | bytes 2097152 | tf_op jit(solution)/shard_map/all_to_all | solution.py:215
  88.2 3.3 collective-permute-start.1
  91.5 3.2 collective-permute-start.2
  94.7 3.6 collective-permute-start.3
  98.9 46.8 %all-to-all-done.3 = bf16[512,8,128]{2,1,0:T(8,128)(2,1)S(1)} async-done(((bf16[512,8,128]{2,1,0:T(8,128)(2,1)}), bf16[512,8,128]{2,1,0:T(8,128)(2,1)S(1)}, u32[]{:S(2)}, u32[]{:S(2)}) %all-to-all-start.3) | async-done | bytes 1048608 | tf_op jit(solution)/shard_map/all_to_all | solution.py:215
  145.7 3.8 collective-permute-done.3.env_3
  149.5 23.6 %middle_stage.2 = bf16[4096,128]{1,0:T(8,128)(2,1)} custom-call(s32[8]{0:T(128)} %stack.50.info, s32[4,128]{1,0:T(4,128)} %bitcast.65, s32[128]{0:T(128)} %row_dims.7, s32[128]{0:T(128)} %col_dims.7, bf16[4096,128]{1,0:T(8,128)(2,1)} %bitcast.56, bf16[4096,128]{1,0:T(8,128)(2,1)} %bitcast.54, bf16[4096,128]{1,0:T(8,128)(2,1)} %copy-done.4, ...), custom_call_target="tpu_custom_call" | custom-call | flops 1073741824 | bytes 6291456 | tf_op jit(solution)/shard_map/middle_stage/pallas_call | solution.py:189
  173.1 21.0 %all-to-all-start.4 = ((bf16[512,8,128]{2,1,0:T(8,128)(2,1)}), bf16[512,8,128]{2,1,0:T(8,128)(2,1)S(1)}, u32[]{:S(2)}, u32[]{:S(2)}) async-start(bf16[512,8,128]{2,1,0:T(8,128)(2,1)} %bitcast.58), calls=%async_computation.4 | async-start | bytes 2097152 | tf_op jit(solution)/shard_map/all_to_all | solution.py:215
  194.2 3.3 collective-permute-start.4
  197.4 3.2 collective-permute-start.5
  200.7 3.6 collective-permute-start.6
  204.2 19.9 %collective-permute-done.4.env_1 = bf16[4096,128]{1,0:T(8,128)(2,1)S(1)} collective-permute-done((bf16[4096,128]{1,0:T(8,128)(2,1)S(1)}, bf16[4096,128]{1,0:T(8,128)(2,1)S(1)}, u32[]{:S(2)}, u32[]{:S(2)}) %collective-permute-start.4) | collective-permute-done | bytes 1048608 | tf_op jit(solution)/shard_map/ppermute | solution.py:239
  224.2 3.8 collective-permute-done.5.env_2
  229.0 26.5 %collective-permute-done.6.env_3 = bf16[4096,128]{1,0:T(8,128)(2,1)} collective-permute-done((bf16[4096,128]{1,0:T(8,128)(2,1)S(1)}, bf16[4096,128]{1,0:T(8,128)(2,1)}, u32[]{:S(2)}, u32[]{:S(2)}) %collective-permute-start.6) | collective-permute-done | bytes 1048608 | tf_op jit(solution)/shard_map/ppermute | solution.py:239
  255.5 1.1 copy-done.3
  256.6 28.2 %middle_stage.3 = bf16[4096,128]{1,0:T(8,128)(2,1)} custom-call(s32[8]{0:T(128)} %stack.50.info, s32[4,128]{1,0:T(4,128)} %bitcast.67, s32[128]{0:T(128)} %col_dims.7, s32[128]{0:T(128)} %row_dims.7, bf16[4096,128]{1,0:T(8,128)(2,1)} %bitcast.57, bf16[4096,128]{1,0:T(8,128)(2,1)} %bitcast.47, bf16[4096,128]{1,0:T(8,128)(2,1)} %copy-done.5, ...), custom_call_target="tpu_custom_call" | custom-call | flops 1073741824 | bytes 6291456 | tf_op jit(solution)/shard_map/middle_stage/pallas_call | solution.py:189
  284.8 79.7 %all_to_all.37 = bf16[512,8,128]{2,1,0:T(8,128)(2,1)} all-to-all(bf16[512,8,128]{2,1,0:T(8,128)(2,1)} %bitcast.59), channel_id=1, replica_groups=mesh['op'=4,'z'=16,'y'=4,'c'=2] {'op','z','y','c'}, dimensions={0} | all-to-all | bytes 2097152 | tf_op jit(solution)/shard_map/all_to_all | solution.py:215
  364.4 19.4 %last_stage.1 = bf16[16,8192]{1,0:T(8,128)(2,1)} custom-call(s32[8]{0:T(128)} %stack.50.info, s32[4,128]{1,0:T(4,128)} %bitcast.66, s32[128]{0:T(128)} %row_dims.7, s32[128]{0:T(128)} %col_dims.7, bf16[4096,128]{1,0:T(8,128)(2,1)} %bitcast.62, bf16[4096,128]{1,0:T(8,128)(2,1)} %bitcast.55, bf16[4096,128]{1,0:T(8,128)(2,1)} %copy-done.4, ...), custom_call_target="tpu_custom_call" | custom-call | flops 1073741824 | bytes 6291456 | tf_op jit(solution)/shard_map/last_stage/pallas_call | solution.py:189
  384.9 17.8 %all_to_all.38 = bf16[4,16,8192]{2,1,0:T(8,128)(2,1)S(1)} all-to-all(bf16[4,16,8192]{2,1,0:T(8,128)(2,1)S(1)} %broadcast_in_dim.15), channel_id=1, replica_groups=mesh['op'=4,'z'=16,'y'=4,'c'=2] {'op'}, dimensions={0} | all-to-all | bytes 2097152 | tf_op jit(solution)/shard_map/all_to_all | solution.py:210
  (44 shorter events, 8.2 us)
Async XLA Ops:
  0.8 0.7 copy-start.7
  44.9 9.0 %copy-start.8 = (s32[1,128]{1,0:T(1,128)S(1)}, s32[1,128]{1,0:T(1,128)}, u32[]{:S(2)}) copy-start(s32[1,128]{1,0:T(1,128)} %param.10) | copy-start | bytes 1540
  44.9 9.0 %copy-start.9 = (s32[1,128]{1,0:T(1,128)S(1)}, s32[1,128]{1,0:T(1,128)}, u32[]{:S(2)}) copy-start(s32[1,128]{1,0:T(1,128)} %param.11) | copy-start | bytes 1540
  45.0 14.3 %collective-permute-start = (bf16[4,16,2,32,128]{4,3,1,0,2:T(8,128)(2,1)S(1)}, bf16[4,16,2,32,128]{4,3,1,0,2:T(8,128)(2,1)S(1)}, u32[]{:S(2)}, u32[]{:S(2)}) collective-permute-start(bf16[4,16,2,32,128]{4,3,1,0,2:T(8,128)(2,1)S(1)} %copy.22), channel_id=1, source_target_pairs={{0,1},{1,0},{2,3},{3,2},{4,5},{5,4},{6,7},{7,6},{8,9},{9,8},{10,11... | collective-permute-start | bytes 3145736 | tf_op jit(solution)/shard_map/ppermute | solution.py:230
  54.6 17.2 %all-to-all-start = ((s32[4,2,128]{2,1,0:T(2,128)}), s32[4,2,128]{2,1,0:T(2,128)S(1)}, u32[]{:S(2)}, u32[]{:S(2)}) async-start(s32[4,2,128]{2,1,0:T(2,128)} %broadcast_in_dim.12), calls=%async_computation | async-start | bytes 8192 | tf_op jit(solution)/shard_map/all_to_all | solution.py:210
  71.7 73.9 %all-to-all-start.3 = ((bf16[512,8,128]{2,1,0:T(8,128)(2,1)}), bf16[512,8,128]{2,1,0:T(8,128)(2,1)S(1)}, u32[]{:S(2)}, u32[]{:S(2)}) async-start(bf16[512,8,128]{2,1,0:T(8,128)(2,1)} %bitcast.61), calls=%async_computation.3 | async-start | bytes 2097152 | tf_op jit(solution)/shard_map/all_to_all | solution.py:215
  88.2 61.3 %copy-start.1 = (bf16[2,4,16,32,128]{4,3,2,1,0:T(8,128)(2,1)}, bf16[2,4,16,32,128]{4,3,2,1,0:T(8,128)(2,1)S(1)}, u32[]{:S(2)}) copy-start(bf16[2,4,16,32,128]{4,3,2,1,0:T(8,128)(2,1)S(1)} %pad_maximum_fusion.1) | copy-start | bytes 3145732
  88.2 57.5 %collective-permute-start.1 = (bf16[4096,128]{1,0:T(8,128)(2,1)S(1)}, bf16[4096,128]{1,0:T(8,128)(2,1)S(1)}, u32[]{:S(2)}, u32[]{:S(2)}) collective-permute-start(bf16[4096,128]{1,0:T(8,128)(2,1)S(1)} %bitcast.51), channel_id=1, source_target_pairs={{0,128},{128,256},{256,384},{384,0},{1,129},{129,257},{257,385},{3... | collective-permute-start | bytes 3145736 | tf_op jit(solution)/shard_map/ppermute | solution.py:239
  91.5 54.2 %collective-permute-start.2 = (bf16[4096,128]{1,0:T(8,128)(2,1)S(1)}, bf16[4096,128]{1,0:T(8,128)(2,1)}, u32[]{:S(2)}, u32[]{:S(2)}) collective-permute-start(bf16[4096,128]{1,0:T(8,128)(2,1)S(1)} %bitcast.52), channel_id=1, source_target_pairs={{0,384},{128,0},{256,128},{384,256},{1,385},{129,1},{257,129},{385... | collective-permute-start | bytes 3145736 | tf_op jit(solution)/shard_map/ppermute | solution.py:239
  94.7 54.8 %collective-permute-start.3 = (bf16[4096,128]{1,0:T(8,128)(2,1)S(1)}, bf16[4096,128]{1,0:T(8,128)(2,1)}, u32[]{:S(2)}, u32[]{:S(2)}) collective-permute-start(bf16[4096,128]{1,0:T(8,128)(2,1)S(1)} %bitcast.53), channel_id=1, source_target_pairs={{0,256},{128,384},{256,0},{384,128},{1,257},{129,385},{257,1},{385... | collective-permute-start | bytes 3145736 | tf_op jit(solution)/shard_map/ppermute | solution.py:239
  145.7 3.8 copy-start.2
  145.7 3.8 copy-start.4
  173.1 21.1 %copy-start = (bf16[2,4,16,32,128]{4,3,2,1,0:T(8,128)(2,1)S(1)}, bf16[2,4,16,32,128]{4,3,2,1,0:T(8,128)(2,1)}, u32[]{:S(2)}) copy-start(bf16[2,4,16,32,128]{4,3,2,1,0:T(8,128)(2,1)} %pad_maximum_fusion) | copy-start | bytes 3145732
  173.1 82.4 %all-to-all-start.4 = ((bf16[512,8,128]{2,1,0:T(8,128)(2,1)}), bf16[512,8,128]{2,1,0:T(8,128)(2,1)S(1)}, u32[]{:S(2)}, u32[]{:S(2)}) async-start(bf16[512,8,128]{2,1,0:T(8,128)(2,1)} %bitcast.58), calls=%async_computation.4 | async-start | bytes 2097152 | tf_op jit(solution)/shard_map/all_to_all | solution.py:215
  194.2 30.0 %collective-permute-start.4 = (bf16[4096,128]{1,0:T(8,128)(2,1)S(1)}, bf16[4096,128]{1,0:T(8,128)(2,1)S(1)}, u32[]{:S(2)}, u32[]{:S(2)}) collective-permute-start(bf16[4096,128]{1,0:T(8,128)(2,1)S(1)} %bitcast.48), channel_id=1, source_target_pairs={{0,128},{128,256},{256,384},{384,0},{1,129},{129,257},{257,385},{3... | collective-permute-start | bytes 3145736 | tf_op jit(solution)/shard_map/ppermute | solution.py:239
  197.4 30.6 %collective-permute-start.5 = (bf16[4096,128]{1,0:T(8,128)(2,1)S(1)}, bf16[4096,128]{1,0:T(8,128)(2,1)S(1)}, u32[]{:S(2)}, u32[]{:S(2)}) collective-permute-start(bf16[4096,128]{1,0:T(8,128)(2,1)S(1)} %bitcast.49), channel_id=1, source_target_pairs={{0,384},{128,0},{256,128},{384,256},{1,385},{129,1},{257,129},{385... | collective-permute-start | bytes 3145736 | tf_op jit(solution)/shard_map/ppermute | solution.py:239
  200.7 54.8 %collective-permute-start.6 = (bf16[4096,128]{1,0:T(8,128)(2,1)S(1)}, bf16[4096,128]{1,0:T(8,128)(2,1)}, u32[]{:S(2)}, u32[]{:S(2)}) collective-permute-start(bf16[4096,128]{1,0:T(8,128)(2,1)S(1)} %bitcast.50), channel_id=1, source_target_pairs={{0,256},{128,384},{256,0},{384,128},{1,257},{129,385},{257,1},{385... | collective-permute-start | bytes 3145736 | tf_op jit(solution)/shard_map/ppermute | solution.py:239
  224.2 31.4 %copy-start.5 = (bf16[4096,128]{1,0:T(8,128)(2,1)}, bf16[4096,128]{1,0:T(8,128)(2,1)S(1)}, u32[]{:S(2)}) copy-start(bf16[4096,128]{1,0:T(8,128)(2,1)S(1)} %collective-permute-done.4.env_1) | copy-start | bytes 3145732
  228.0 1.0 copy-start.6
  255.5 1.1 copy-start.3

commit v2 on v1

--- a/solution.py
+++ b/solution.py
@@ -21,7 +21,7 @@
 def spot(info, sizes, sector):
     nz, ny = sizes
     core, rest = sector & 1, sector >> 1
-    return ((core ^ info[2]) * ny + lax.rem(rest, ny)) * nz + lax.div(rest, ny)
+    return ((core ^ info[2]) * ny + (rest & (ny - 1))) * nz + (rest >> (ny.bit_length() - 1))
 
 
 def fold_out(out_ref, pair, count, first, second):
@@ -45,7 +45,7 @@
         blocks[2 * pair + 1] = jnp.where(low, turned, value).astype(BF16)
         return carry
 
-    lax.fori_loop(0, count // 2, spread, 0, unroll=2)
+    lax.fori_loop(0, count // 2, spread, 0, unroll=16)
     zero = jnp.zeros((64, 128), BF16)
 
     def product(block):
@@ -59,7 +59,7 @@
         fold_out(out, pair, count, product(2 * pair), product(2 * pair + 1))
         return carry
 
-    lax.fori_loop(0, count // 2, step, 0, unroll=2)
+    lax.fori_loop(0, count // 2, step, 0, unroll=16)
 
 
 def middle_kernel(
@@ -99,7 +99,7 @@
                 tiles[w, 2 * pair + k] = tile.astype(BF16)
         return carry
 
-    lax.fori_loop(0, count // 2, place, 0, unroll=2)
+    lax.fori_loop(0, count // 2, place, 0, unroll=16)
     for copy in copies:
         copy.wait()
 
@@ -134,7 +134,7 @@
             out[:, pl.ds(pl.multiple_of(pair * 128, 128), 128)] = value.astype(BF16)
             return carry
 
-        lax.fori_loop(0, count // 2, finish, 0, unroll=2)
+        lax.fori_loop(0, count // 2, finish, 0, unroll=16)
         return
 
     def keep(block, carry):
@@ -144,7 +144,7 @@
         held[block] = jnp.concatenate([first, first, second, second], axis=0).astype(BF16)
         return carry
 
-    lax.fori_loop(0, count, keep, 0, unroll=4)
+    lax.fori_loop(0, count, keep, 0, unroll=32)
     masks = [[(upper if p == 0 else ~upper) & (low if h == 0 else ~low) for h in range(2)] for p in range(2)]
 
     def product(block):
@@ -164,7 +164,7 @@
         fold_out(out, pair, count, product(2 * pair), product(2 * pair + 1))
         return carry
 
-    lax.fori_loop(0, count // 2, step, 0, unroll=2)
+    lax.fori_loop(0, count // 2, step, 0, unroll=16)
 
 
 SMEM = pl.BlockSpec(memory_space=pltpu.SMEM)
@@ -179,6 +179,7 @@
         in_specs=[SMEM] * 4 + [VMEM] * 2,
         out_specs=VMEM,
         scratch_shapes=[pltpu.VMEM((count, 64, 128), BF16)],
+        compiler_params=pltpu.CompilerParams(vmem_limit_bytes=16 * 2**20),
         cost_estimate=pl.CostEstimate(flops=count * 2**20, bytes_accessed=count * 24576, transcendentals=0),
         name="left_stage",
     )(info, source, row_dims, col_dims, wave, env)
@@ -197,6 +198,7 @@
             pltpu.VMEM((count, 32, 128), BF16),
             pltpu.SemaphoreType.DMA((4,)),
         ],
+        compiler_params=pltpu.CompilerParams(vmem_limit_bytes=24 * 2**20),
         cost_estimate=pl.CostEstimate(flops=count * 2**23, bytes_accessed=count * 49152, transcendentals=0),
         name="last_stage" if last else "middle_stage",
     )(info, source, row_dims, col_dims, arrived, *envs)

time: 405 us -> 358 us (0.88)
  Pallas kernels: 82.5 us -> 31.2 us
  local copies, waits for them, and re-layouts: 7.97 us -> 14.3 us
    pallas_call x3, Pallas kernels: 71.2 us -> 26.4 us  [middle_stage(): pl.pallas_call(functools.partial(middle_kernel, count, sizes, turn, last)...]
    unnamed x21 -> x29, local copies, waits for them, and re-layouts: 3.58 us -> 11.2 us
    pallas_call x1, Pallas kernels: 11.3 us -> 4.79 us  [left_stage(): pl.pallas_call(functools.partial(left_kernel, count, sizes), out_shape=ja...]
  transfers between devices with their start and end apart: 10 -> 10, of which waited for: 5 -> 5; matrix products, arithmetic and copies ran while one was open for 1% -> 1% of each run, Pallas kernels for 3% -> 1%
where the time goes in v2:
time: 358 us; the launch traced here: 357 us
  blocking collectives  140 us (39%)
  waiting for transfers between devices  100 us (28%)
  starting transfers between devices  70.2 us (20%)
  Pallas kernels  31.2 us (9%)
  local copies, waits for them, and re-layouts  14.3 us (4%)
    all_to_all x1, blocking collectives, exchange(): lax.all_to_all(chunks.reshape(devices, 8, 128), ALL, 0, 0, tiled=True)  79.5 us
    all_to_all x3, blocking collectives, copies_to(): lax.all_to_all(jnp.broadcast_to(value, (size,) + value.shape), axis, 0, 0...  60.8 us
    ppermute x6, waiting for transfers between devices, over_op(): lax.ppermute(value, 'op', [(i, (i + s) % 4) for i in range(4)])  53.9 us
    all_to_all x2, waiting for transfers between devices, exchange(): lax.all_to_all(chunks.reshape(devices, 8, 128), ALL, 0, 0, tiled=True)  46.4 us
    all_to_all x2, starting transfers between devices, exchange(): lax.all_to_all(chunks.reshape(devices, 8, 128), ALL, 0, 0, tiled=True)  37.2 us
    pallas_call x3, Pallas kernels, middle_stage(): pl.pallas_call(functools.partial(middle_kernel, count, sizes, turn, last)...  26.4 us
    ppermute x6, starting transfers between devices, over_op(): lax.ppermute(value, 'op', [(i, (i + s) % 4) for i in range(4)])  20.1 us
    unnamed x29, local copies, waits for them, and re-layouts  11.2 us
  transfers between devices with their start and end apart: 10, of which 5 were waited for; matrix products, arithmetic and copies ran while one was open for 1% of the time, Pallas kernels for 1%

profile of v2, /device:TPU:1, one launch (start us, length us, event | category | flops | bytes accessed | tf_op | source)
XLA Modules:
  0.0 356.9 jit_solution(3192304349799133894)
XLA Ops:
  1.7 29.3 %all_to_all.35 = bf16[16,2,32,128]{3,2,1,0:T(8,128)(2,1)S(1)} all-to-all(bf16[16,2,32,128]{3,2,1,0:T(8,128)(2,1)S(1)} %broadcast_in_dim.13), channel_id=1, replica_groups=mesh['op'=4,'z'=16,'y'=4,'c'=2] {'z'}, dimensions={0} | all-to-all | bytes 524288 | tf_op jit(solution)/shard_map/all_to_all | solution.py:212
  31.2 13.7 %all_to_all.36 = bf16[4,16,2,32,128]{4,3,1,2,0:T(8,128)(2,1)S(1)} all-to-all(bf16[4,16,2,32,128]{4,3,1,2,0:T(8,128)(2,1)S(1)} %broadcast_in_dim.14), channel_id=1, replica_groups=mesh['op'=4,'z'=16,'y'=4,'c'=2] {'y'}, dimensions={0} | all-to-all | bytes 2097152 | tf_op jit(solution)/shard_map/all_to_all | solution.py:212
  45.0 8.9 %collective-permute-start = (bf16[4,16,2,32,128]{4,3,1,0,2:T(8,128)(2,1)S(1)}, bf16[4,16,2,32,128]{4,3,1,0,2:T(8,128)(2,1)S(1)}, u32[]{:S(2)}, u32[]{:S(2)}) collective-permute-start(bf16[4,16,2,32,128]{4,3,1,0,2:T(8,128)(2,1)S(1)} %copy.22), channel_id=1, source_target_pairs={{0,1},{1,0},{2,3},{3,2},{4,5},{5,4},{6,7},{7,6},{8,9},{9,8},{10,11... | collective-permute-start | bytes 3145736 | tf_op jit(solution)/shard_map/ppermute | solution.py:232
  54.5 4.0 %all-to-all-start = ((s32[4,2,128]{2,1,0:T(2,128)}), s32[4,2,128]{2,1,0:T(2,128)S(1)}, u32[]{:S(2)}, u32[]{:S(2)}) async-start(s32[4,2,128]{2,1,0:T(2,128)} %broadcast_in_dim.12), calls=%async_computation | async-start | bytes 8192 | tf_op jit(solution)/shard_map/all_to_all | solution.py:212
  60.8 4.8 %left_stage.1 = bf16[4096,128]{1,0:T(8,128)(2,1)} custom-call(s32[8]{0:T(128)S(1)} %stack.50.info, s32[128]{0:T(128)S(1)} %bitcast.65, s32[128]{0:T(128)S(1)} %copy-done.8, s32[128]{0:T(128)S(1)} %copy-done.9, bf16[64,8192]{1,0:T(8,128)(2,1)S(1)} %bitcast.61, bf16[4096,128]{1,0:T(8,128)(2,1)S(1)} %bitcast.46), custom_call_target="tpu_custom_call" | custom-call | flops 134217728 | bytes 3145728 | tf_op jit(solution)/shard_map/left_stage/pallas_call | solution.py:176
  65.6 16.3 %all-to-all-start.3 = ((bf16[512,8,128]{2,1,0:T(8,128)(2,1)}), bf16[512,8,128]{2,1,0:T(8,128)(2,1)S(1)}, u32[]{:S(2)}, u32[]{:S(2)}) async-start(bf16[512,8,128]{2,1,0:T(8,128)(2,1)} %bitcast.21), calls=%async_computation.3 | async-start | bytes 2097152 | tf_op jit(solution)/shard_map/all_to_all | solution.py:217
  83.0 3.3 collective-permute-start.1
  86.3 3.2 collective-permute-start.2
  89.6 3.6 collective-permute-start.3
  93.1 46.4 %all-to-all-done.3 = bf16[512,8,128]{2,1,0:T(8,128)(2,1)S(1)} async-done(((bf16[512,8,128]{2,1,0:T(8,128)(2,1)}), bf16[512,8,128]{2,1,0:T(8,128)(2,1)S(1)}, u32[]{:S(2)}, u32[]{:S(2)}) %all-to-all-start.3) | async-done | bytes 1048608 | tf_op jit(solution)/shard_map/all_to_all | solution.py:217
  139.5 4.7 %collective-permute-done.3.env_3 = bf16[4096,128]{1,0:T(8,128)(2,1)} collective-permute-done((bf16[4096,128]{1,0:T(8,128)(2,1)S(1)}, bf16[4096,128]{1,0:T(8,128)(2,1)}, u32[]{:S(2)}, u32[]{:S(2)}) %collective-permute-start.3) | collective-permute-done | bytes 1048608 | tf_op jit(solution)/shard_map/ppermute | solution.py:241
  144.3 9.8 %middle_stage.2 = bf16[4096,128]{1,0:T(8,128)(2,1)S(1)} custom-call(s32[8]{0:T(128)S(1)} %stack.50.info, s32[4,128]{1,0:T(4,128)S(1)} %bitcast.62, s32[128]{0:T(128)S(1)} %copy-done.8, s32[128]{0:T(128)S(1)} %copy-done.9, bf16[4096,128]{1,0:T(8,128)(2,1)S(1)} %bitcast.56, bf16[4096,128]{1,0:T(8,128)(2,1)S(1)} %bitcast.54, ...), custom_call_target="tpu_custom_call" | custom-call | flops 1073741824 | bytes 6291456 | tf_op jit(solution)/shard_map/middle_stage/pallas_call | solution.py:190
  155.1 20.9 %all-to-all-start.4 = ((bf16[512,8,128]{2,1,0:T(8,128)(2,1)}), bf16[512,8,128]{2,1,0:T(8,128)(2,1)S(1)}, u32[]{:S(2)}, u32[]{:S(2)}) async-start(bf16[512,8,128]{2,1,0:T(8,128)(2,1)} %bitcast.58), calls=%async_computation.4 | async-start | bytes 2097152 | tf_op jit(solution)/shard_map/all_to_all | solution.py:217
  176.0 3.3 collective-permute-start.4
  179.3 3.2 collective-permute-start.5
  182.5 3.6 collective-permute-start.6
  186.1 19.9 %collective-permute-done.4.env_1 = bf16[4096,128]{1,0:T(8,128)(2,1)S(1)} collective-permute-done((bf16[4096,128]{1,0:T(8,128)(2,1)S(1)}, bf16[4096,128]{1,0:T(8,128)(2,1)S(1)}, u32[]{:S(2)}, u32[]{:S(2)}) %collective-permute-start.4) | collective-permute-done | bytes 1048608 | tf_op jit(solution)/shard_map/ppermute | solution.py:241
  207.0 2.9 collective-permute-done.5.env_2
  210.9 26.4 %collective-permute-done.6.env_3 = bf16[4096,128]{1,0:T(8,128)(2,1)S(1)} collective-permute-done((bf16[4096,128]{1,0:T(8,128)(2,1)S(1)}, bf16[4096,128]{1,0:T(8,128)(2,1)S(1)}, u32[]{:S(2)}, u32[]{:S(2)}) %collective-permute-start.6) | collective-permute-done | bytes 1048608 | tf_op jit(solution)/shard_map/ppermute | solution.py:241
  238.2 1.2 copy-done.2
  241.9 10.8 %middle_stage.3 = bf16[4096,128]{1,0:T(8,128)(2,1)S(1)} custom-call(s32[8]{0:T(128)S(1)} %stack.50.info, s32[4,128]{1,0:T(4,128)S(1)} %bitcast.64, s32[128]{0:T(128)S(1)} %copy-done.9, s32[128]{0:T(128)S(1)} %copy-done.8, bf16[4096,128]{1,0:T(8,128)(2,1)S(1)} %bitcast.57, bf16[4096,128]{1,0:T(8,128)(2,1)S(1)} %bitcast.50, bf16[4096,128]{1,0:T(8,128)(2,1)S(1)} %copy-done.2, ...), custom_call_target="tpu_custom_call" | custom-call | flops 1073741824 | bytes 6291456 | tf_op jit(solution)/shard_map/middle_stage/pallas_call | solution.py:190
  252.7 79.5 %all_to_all.37 = bf16[512,8,128]{2,1,0:T(8,128)(2,1)S(1)} all-to-all(bf16[512,8,128]{2,1,0:T(8,128)(2,1)S(1)} %bitcast.59), channel_id=1, replica_groups=mesh['op'=4,'z'=16,'y'=4,'c'=2] {'op','z','y','c'}, dimensions={0} | all-to-all | bytes 2097152 | tf_op jit(solution)/shard_map/all_to_all | solution.py:217
  332.2 5.7 %last_stage.1 = bf16[16,8192]{1,0:T(8,128)(2,1)S(1)} custom-call(s32[8]{0:T(128)S(1)} %stack.50.info, s32[4,128]{1,0:T(4,128)S(1)} %bitcast.63, s32[128]{0:T(128)S(1)} %copy-done.8, s32[128]{0:T(128)S(1)} %copy-done.9, bf16[4096,128]{1,0:T(8,128)(2,1)S(1)} %bitcast.60, bf16[4096,128]{1,0:T(8,128)(2,1)S(1)} %bitcast.55, ...), custom_call_target="tpu_custom_call" | custom-call | flops 1073741824 | bytes 6291456 | tf_op jit(solution)/shard_map/last_stage/pallas_call | solution.py:190
  338.1 17.8 %all_to_all.38 = bf16[4,16,8192]{2,1,0:T(8,128)(2,1)S(1)} all-to-all(bf16[4,16,8192]{2,1,0:T(8,128)(2,1)S(1)} %broadcast_in_dim.15), channel_id=1, replica_groups=mesh['op'=4,'z'=16,'y'=4,'c'=2] {'op'}, dimensions={0} | all-to-all | bytes 2097152 | tf_op jit(solution)/shard_map/all_to_all | solution.py:212
  (52 shorter events, 13.4 us)
Async XLA Ops:
  0.8 0.7 copy-start.12
  44.9 9.0 %copy-start.10 = (s32[1,128]{1,0:T(1,128)S(1)}, s32[1,128]{1,0:T(1,128)}, u32[]{:S(2)}) copy-start(s32[1,128]{1,0:T(1,128)} %param.10) | copy-start | bytes 1540
  44.9 9.0 %copy-start.13 = (s32[1,128]{1,0:T(1,128)S(1)}, s32[1,128]{1,0:T(1,128)}, u32[]{:S(2)}) copy-start(s32[1,128]{1,0:T(1,128)} %param.11) | copy-start | bytes 1540
  45.0 13.7 %collective-permute-start = (bf16[4,16,2,32,128]{4,3,1,0,2:T(8,128)(2,1)S(1)}, bf16[4,16,2,32,128]{4,3,1,0,2:T(8,128)(2,1)S(1)}, u32[]{:S(2)}, u32[]{:S(2)}) collective-permute-start(bf16[4,16,2,32,128]{4,3,1,0,2:T(8,128)(2,1)S(1)} %copy.22), channel_id=1, source_target_pairs={{0,1},{1,0},{2,3},{3,2},{4,5},{5,4},{6,7},{7,6},{8,9},{9,8},{10,11... | collective-permute-start | bytes 3145736 | tf_op jit(solution)/shard_map/ppermute | solution.py:232
  54.5 11.1 %all-to-all-start = ((s32[4,2,128]{2,1,0:T(2,128)}), s32[4,2,128]{2,1,0:T(2,128)S(1)}, u32[]{:S(2)}, u32[]{:S(2)}) async-start(s32[4,2,128]{2,1,0:T(2,128)} %broadcast_in_dim.12), calls=%async_computation | async-start | bytes 8192 | tf_op jit(solution)/shard_map/all_to_all | solution.py:212
  59.6 1.2 copy-start.7
  59.7 1.1 copy-start.8
  59.7 1.1 copy-start.9
  65.6 73.9 %all-to-all-start.3 = ((bf16[512,8,128]{2,1,0:T(8,128)(2,1)}), bf16[512,8,128]{2,1,0:T(8,128)(2,1)S(1)}, u32[]{:S(2)}, u32[]{:S(2)}) async-start(bf16[512,8,128]{2,1,0:T(8,128)(2,1)} %bitcast.21), calls=%async_computation.3 | async-start | bytes 2097152 | tf_op jit(solution)/shard_map/all_to_all | solution.py:217
  81.9 1.0 copy-start.11
  83.0 56.5 %collective-permute-start.1 = (bf16[4096,128]{1,0:T(8,128)(2,1)S(1)}, bf16[4096,128]{1,0:T(8,128)(2,1)}, u32[]{:S(2)}, u32[]{:S(2)}) collective-permute-start(bf16[4096,128]{1,0:T(8,128)(2,1)S(1)} %bitcast.51), channel_id=1, source_target_pairs={{0,128},{128,256},{256,384},{384,0},{1,129},{129,257},{257,385},{3... | collective-permute-start | bytes 3145736 | tf_op jit(solution)/shard_map/ppermute | solution.py:241
  86.3 53.2 %collective-permute-start.2 = (bf16[4096,128]{1,0:T(8,128)(2,1)S(1)}, bf16[4096,128]{1,0:T(8,128)(2,1)}, u32[]{:S(2)}, u32[]{:S(2)}) collective-permute-start(bf16[4096,128]{1,0:T(8,128)(2,1)S(1)} %bitcast.52), channel_id=1, source_target_pairs={{0,384},{128,0},{256,128},{384,256},{1,385},{129,1},{257,129},{385... | collective-permute-start | bytes 3145736 | tf_op jit(solution)/shard_map/ppermute | solution.py:241
  89.6 54.7 %collective-permute-start.3 = (bf16[4096,128]{1,0:T(8,128)(2,1)S(1)}, bf16[4096,128]{1,0:T(8,128)(2,1)}, u32[]{:S(2)}, u32[]{:S(2)}) collective-permute-start(bf16[4096,128]{1,0:T(8,128)(2,1)S(1)} %bitcast.53), channel_id=1, source_target_pairs={{0,256},{128,384},{256,0},{384,128},{1,257},{129,385},{257,1},{385... | collective-permute-start | bytes 3145736 | tf_op jit(solution)/shard_map/ppermute | solution.py:241
  154.1 1.0 copy-start
  155.1 83.2 %all-to-all-start.4 = ((bf16[512,8,128]{2,1,0:T(8,128)(2,1)}), bf16[512,8,128]{2,1,0:T(8,128)(2,1)S(1)}, u32[]{:S(2)}, u32[]{:S(2)}) async-start(bf16[512,8,128]{2,1,0:T(8,128)(2,1)} %bitcast.58), calls=%async_computation.4 | async-start | bytes 2097152 | tf_op jit(solution)/shard_map/all_to_all | solution.py:217
  176.0 30.0 %collective-permute-start.4 = (bf16[4096,128]{1,0:T(8,128)(2,1)S(1)}, bf16[4096,128]{1,0:T(8,128)(2,1)S(1)}, u32[]{:S(2)}, u32[]{:S(2)}) collective-permute-start(bf16[4096,128]{1,0:T(8,128)(2,1)S(1)} %bitcast.47), channel_id=1, source_target_pairs={{0,128},{128,256},{256,384},{384,0},{1,129},{129,257},{257,385},{3... | collective-permute-start | bytes 3145736 | tf_op jit(solution)/shard_map/ppermute | solution.py:241
  179.3 30.6 %collective-permute-start.5 = (bf16[4096,128]{1,0:T(8,128)(2,1)S(1)}, bf16[4096,128]{1,0:T(8,128)(2,1)S(1)}, u32[]{:S(2)}, u32[]{:S(2)}) collective-permute-start(bf16[4096,128]{1,0:T(8,128)(2,1)S(1)} %bitcast.48), channel_id=1, source_target_pairs={{0,384},{128,0},{256,128},{384,256},{1,385},{129,1},{257,129},{385... | collective-permute-start | bytes 3145736 | tf_op jit(solution)/shard_map/ppermute | solution.py:241
  182.5 54.7 %collective-permute-start.6 = (bf16[4096,128]{1,0:T(8,128)(2,1)S(1)}, bf16[4096,128]{1,0:T(8,128)(2,1)S(1)}, u32[]{:S(2)}, u32[]{:S(2)}) collective-permute-start(bf16[4096,128]{1,0:T(8,128)(2,1)S(1)} %bitcast.49), channel_id=1, source_target_pairs={{0,256},{128,384},{256,0},{384,128},{1,257},{129,385},{257,1},{385... | collective-permute-start | bytes 3145736 | tf_op jit(solution)/shard_map/ppermute | solution.py:241
  206.0 1.0 copy-start.1
  209.8 1.0 copy-start.3
  237.2 1.0 copy-start.5
  238.2 1.2 copy-start.2
  239.5 1.2 copy-start.4
  240.7 1.2 copy-start.6

commit v3 on v2

v3 whole, which is shorter than its diff:
```python
import functools

import jax
import jax.numpy as jnp
from jax import lax
from jax.experimental import pallas as pl
from jax.experimental.pallas import tpu as pltpu
from jax.sharding import Mesh
from jax.sharding import PartitionSpec as P

BF16, F32 = jnp.bfloat16, jnp.float32
NT = (((1,), (1,)), ((), ()))
SEC = ("z", "y", "c")
ALL = ("op",) + SEC


def iota(shape, axis):
    return lax.broadcasted_iota(jnp.int32, shape, axis)


def spot(info, sizes, sector):
    nz, ny = sizes
    core, rest = sector & 1, sector >> 1
    return ((core ^ info[2]) * ny + (rest & (ny - 1))) * nz + (rest >> (ny.bit_length() - 1))


def fold_out(out_ref, pair, count, first, second):
    for q in range(4):
        rows = jnp.concatenate([first[8 * q : 8 * q + 8], second[8 * q : 8 * q + 8]], axis=0)
        start = pl.multiple_of(q * count * 8 + pair * 16, 16)
        out_ref[pl.ds(start, 16), :] = rows.astype(BF16)


def pack(dense, start, value):
    dense[pl.ds(start, 32), :] = value
    dense[pl.ds(start + 32, 32), :] = pltpu.roll(value, 64, 1)


def send_packed(dense, out, owners):
    low = iota((16, 128), 1) < 64

    def narrow(step, carry):
        start = pl.multiple_of(step * 16, 16)
        even = dense[pl.ds(start * 2, 16, stride=2), :]
        odd = pltpu.roll(dense[pl.ds(start * 2 + 1, 16, stride=2), :], 64, 1)
        out[pl.ds(start, 16), :] = jnp.where(low, even, odd).astype(BF16)
        return carry

    lax.fori_loop(0, owners * 6 // 16, narrow, 0, unroll=16 if owners > 32 else 1)


def left_kernel(
    count, sizes, info, source, row_dims, col_dims, row_at, wave, env, out, blocks, dense
):
    lane = iota((64, 128), 1)
    low = lane < 64
    alive = iota((64, 128), 0) < col_dims[info[1]]

    def spread(pair, carry):
        value = wave[:, pl.ds(pl.multiple_of(pair * 128, 128), 128)].astype(F32)
        extent = jnp.where(low, row_dims[2 * pair], row_dims[2 * pair + 1] + 64)
        value = jnp.where(alive & (lane < extent), value, 0.0)
        turned = pltpu.roll(value, 64, 1)
        blocks[2 * pair] = jnp.where(low, value, turned).astype(BF16)
        blocks[2 * pair + 1] = jnp.where(low, turned, value).astype(BF16)
        return carry

    lax.fori_loop(0, count // 2, spread, 0, unroll=min(16, count // 2))
    zero = jnp.zeros((64, 128), BF16)

    def product(block):
        place = spot(info, sizes, block)
        e = env[pl.ds(pl.multiple_of(place * 32, 32), 32), :]
        f = blocks[source[block]]
        rhs = jnp.concatenate([jnp.where(low, f, zero), jnp.where(low, zero, f)], axis=0)
        return lax.dot_general(e, rhs, NT, preferred_element_type=F32)

    def group(step, carry):
        values = [product(step * 8 + i) for i in range(8)]
        for i in range(8):
            pack(dense, row_at[step * 8 + i], values[i])
        return carry

    lax.fori_loop(0, count // 8, group, 0, unroll=min(8, count // 8))
    send_packed(dense, out, count * 4)


def middle_kernel(
    count, sizes, turn, last, info, source, row_dims, col_dims, col_at,
    arrived, env_0, env_1, env_3, env_2a, env_2b, out, env, tiles, held, wide, dense, padded, offsets, sems,
):
    half_env = count * 16
    copies = [
        pltpu.make_async_copy(env_0, env.at[info[3]], sems.at[0]),
        pltpu.make_async_copy(env_1, env.at[info[4]], sems.at[1]),
        pltpu.make_async_copy(env_3, env.at[info[5]], sems.at[2]),
        pltpu.make_async_copy(env_2a, env.at[info[6], pl.ds(0, half_env)], sems.at[3]),
        pltpu.make_async_copy(env_2b, env.at[info[6], pl.ds(half_env, half_env)], sems.at[4]),
    ]
    for copy in copies:
        copy.start()
    lane8 = iota((8, 128), 1)
    low8 = lane8 < 64
    rows_in = 8 if last else 6
    total_rows = arrived.shape[0]

    def widen(step, carry):
        start = pl.multiple_of(step * 16, 16)
        wide[pl.ds(start, 16), :] = arrived[pl.ds(start, 16), :].astype(F32)
        return carry

    lax.fori_loop(0, total_rows // 16, widen, 0, unroll=16 if count > 8 else 1)
    wide[pl.ds(total_rows, 8), :] = jnp.zeros((8, 128), F32)


    def settle(w, block, value):
        turned = pltpu.roll(value, 64, 1)
        first, second = jnp.where(low8, value, turned), jnp.where(low8, turned, value)
        tiles[w, block] = jnp.concatenate([first, second], axis=0).astype(BF16)

    if turn:
        bit0, bit1 = (lane8 & 16) == 0, (lane8 & 32) == 0
        zero_tile = jnp.zeros((16, 128), BF16)
        for w in range(4):
            padded[w, count // 2] = zero_tile
        spot_of = iota((256, 128), 0)
        number = (spot_of >> 4) * 12 + (spot_of & 7) * 2 + ((spot_of >> 3) & 1)
        offsets[...] = jnp.where((spot_of & 7) < 6, number, -4096) - (iota((256, 128), 1) & 63)

        def regroup(e, carry):
            sets = []
            for k in range(2):
                got = [wide[pl.ds((8 * e + 4 * k + x) * rows_in, 8), :] for x in range(4)]
                for a, b in ((0, 1), (2, 3)):
                    one, two = got[a], got[b]
                    got[a] = jnp.where(bit0, one, pltpu.roll(two, 16, 1))
                    got[b] = jnp.where(bit0, pltpu.roll(one, 112, 1), two)
                for a, b in ((0, 2), (1, 3)):
                    one, two = got[a], got[b]
                    got[a] = jnp.where(bit1, one, pltpu.roll(two, 32, 1))
                    got[b] = jnp.where(bit1, pltpu.roll(one, 96, 1), two)
                sets.append(got)
            for w in range(4):
                one, two = sets[0][w], sets[1][w]
                first = jnp.where(low8, one, pltpu.roll(two, 64, 1))
                second = jnp.where(low8, pltpu.roll(one, 64, 1), two)
                padded[w, e] = jnp.concatenate([first, second], axis=0).astype(BF16)
            return carry

        lax.fori_loop(0, count // 2, regroup, 0, unroll=min(8, count // 2))
        lane_k = iota((256, 128), 1) & 63

        def place(block, carry):
            at = col_at[block]
            f = lax.div(at, 96)
            pick = (offsets[...] == at - f * 96) & (lane_k < col_dims[block])
            pick = jnp.where(pick, 1.0, 0.0).astype(BF16)
            lhs = [jnp.concatenate([padded[w, f], padded[w, f + 1]], axis=1) for w in range(4)]
            lhs = jnp.concatenate(lhs, axis=0)
            value = jnp.dot(lhs, pick, preferred_element_type=F32).astype(BF16)
            for w in range(4):
                tiles[w, block] = value[16 * w : 16 * w + 16]
            return carry
    else:

        def place(block, carry):
            for w in range(4):
                settle(w, block, wide[pl.ds((w * count + block) * rows_in, 8), :])
            return carry

    lax.fori_loop(0, count, place, 0, unroll=min(16, count))
    for copy in copies:
        copy.wait()

    low = iota((16, 128), 1) < 64
    zero = jnp.zeros((16, 128), BF16)
    pad = jnp.zeros((32, 96), F32)
    lane_in = iota((16, 128), 1) & 63
    if last:
        row = iota((16, 128), 0)
        natural = (row & 7) + (row >> 3) * 32 + info[0] * 8
        row_alive = natural < row_dims[info[1]]

    def env_of(block):
        start = pl.multiple_of(spot(info, sizes, block) * 32, 32)
        return jnp.concatenate([env[w, pl.ds(start, 32), :] for w in range(4)], axis=1)

    def summed(block):
        lhs = []
        for w in range(4):
            t = tiles[w, source[w, block]]
            lhs.append(jnp.concatenate([jnp.where(low, t, zero), jnp.where(low, zero, t)], axis=0))
        lhs = jnp.concatenate(lhs, axis=1)
        total = lax.dot_general(lhs, env_of(block), NT, preferred_element_type=F32)
        total = jnp.concatenate([total, pad], axis=1)
        total = total[:16] + pltpu.roll(total[16:], 32, 1)
        alive = lane_in < col_dims[block]
        return jnp.where(row_alive & alive if last else alive, total, 0.0)

    if last:

        def finish(pair, carry):
            value = summed(2 * pair) + pltpu.roll(summed(2 * pair + 1), 64, 1)
            out[:, pl.ds(pl.multiple_of(pair * 128, 128), 128)] = value.astype(BF16)
            return carry

        lax.fori_loop(0, count // 2, finish, 0, unroll=min(16, count // 2))
        return

    def keep(block, carry):
        value = summed(block)
        held[block] = (value + pltpu.roll(value, 64, 1)).astype(BF16)
        return carry

    lax.fori_loop(0, count, keep, 0, unroll=min(32, count))

    def product(block):
        slots = []
        for w in range(4):
            both = held[source[w, block]]
            rows = []
            for h in range(2):
                tile = jnp.where(low, both, zero) if h == 0 else jnp.where(low, zero, both)
                rows += [tile if v == w else zero for v in range(4)]
            slots.append(jnp.concatenate(rows, axis=0))
        rhs = jnp.concatenate(slots, axis=1)
        return lax.dot_general(env_of(block), rhs, NT, preferred_element_type=F32)

    if turn:

        def step(pair, carry):
            fold_out(out, pair, count, product(2 * pair), product(2 * pair + 1))
            return carry

        lax.fori_loop(0, count // 2, step, 0, unroll=min(16, count // 2))
        return

    def group(step, carry):
        values = [product(step * 8 + i) for i in range(8)]
        for i in range(8):
            pack(dense, col_at[step * 8 + i], values[i])
        return carry

    lax.fori_loop(0, count // 8, group, 0, unroll=min(8, count // 8))
    send_packed(dense, out, count * 4)


SMEM = pl.BlockSpec(memory_space=pltpu.SMEM)
VMEM = pl.BlockSpec(memory_space=pltpu.VMEM)
ANY = pl.BlockSpec(memory_space=pl.ANY)


def left_stage(count, sizes, info, source, row_dims, col_dims, row_at, wave, env):
    return pl.pallas_call(
        functools.partial(left_kernel, count, sizes),
        out_shape=jax.ShapeDtypeStruct((count * 24, 128), BF16),
        in_specs=[SMEM] * 5 + [VMEM] * 2,
        out_specs=VMEM,
        scratch_shapes=[
            pltpu.VMEM((count, 64, 128), BF16),
            pltpu.VMEM((count * 48 + 64, 128), F32),
        ],
        compiler_params=pltpu.CompilerParams(vmem_limit_bytes=20 * 2**20),
        cost_estimate=pl.CostEstimate(flops=count * 2**20, bytes_accessed=count * 24576, transcendentals=0),
        name="left_stage",
    )(info, source, row_dims, col_dims, row_at, wave, env)


def middle_stage(count, sizes, turn, last, info, source, row_dims, col_dims, col_at, arrived, envs):
    shape = (16, count * 64) if last else (count * (32 if turn else 24), 128)
    return pl.pallas_call(
        functools.partial(middle_kernel, count, sizes, turn, last),
        out_shape=jax.ShapeDtypeStruct(shape, BF16),
        in_specs=[SMEM] * 5 + [VMEM] + [ANY] * 5,
        out_specs=VMEM,
        scratch_shapes=[
            pltpu.VMEM((4, count * 32, 128), BF16),
            pltpu.VMEM((4, count, 16, 128), BF16),
            pltpu.VMEM((count, 16, 128), BF16),
            pltpu.VMEM((count * 32 + 8, 128), F32),
            pltpu.VMEM((count * 48 + 64, 128), F32),
            pltpu.VMEM((4, count // 2 + 1, 16, 128), BF16),
            pltpu.VMEM((256, 128), jnp.int32),
            pltpu.SemaphoreType.DMA((5,)),
        ],
        compiler_params=pltpu.CompilerParams(vmem_limit_bytes=26 * 2**20),
        cost_estimate=pl.CostEstimate(flops=count * 2**23, bytes_accessed=count * 49152, transcendentals=0),
        name="last_stage" if last else "middle_stage",
    )(info, source, row_dims, col_dims, col_at, arrived, *envs)


def fold(block):
    return jnp.concatenate([block[:32], block[32:]], axis=1)


def copies_to(value, axis, size):
    return lax.all_to_all(jnp.broadcast_to(value, (size,) + value.shape), axis, 0, 0, tiled=True)


def exchange(chunks, devices):
    shape = chunks.shape
    pieces = chunks.reshape(devices, shape[0] // devices // 2, 2, 128)
    return lax.all_to_all(pieces, ALL, 0, 0, tiled=True).reshape(shape)


def on_device(sizes, wave, left_env, right_env, left_map, right_map, left_dims, right_dims):
    nz, ny = sizes
    count = left_map.shape[1]
    me, core = lax.axis_index("op"), lax.axis_index("c")
    sector = lax.axis_index(SEC)
    shifts = (0, 1, 3, 2)
    starts = [jnp.cumsum(d) - d for d in (left_dims, right_dims)]
    info = jnp.stack([me, sector, core] + [lax.rem(me + 4 - s, 4) for s in shifts] + [me]).astype(jnp.int32)

    maps = copies_to(jnp.stack([left_map[0], right_map[0]]), "op", 4)
    own = jnp.stack([fold(left_env[0, 0]), fold(right_env[0, 0].T)])
    over_z = copies_to(own, "z", nz)
    over_y = copies_to(over_z, "y", ny)
    other = lax.ppermute(over_y, "c", [(0, 1), (1, 0)])

    def gathered(which):
        both = jnp.stack([over_y[:, :, which], other[:, :, which]])
        return both.reshape(count * 32, 128)

    left_own, right_own = gathered(0), gathered(1)

    def over_op(value):
        half = count * 16
        ahead = lax.ppermute(value, "op", [(i, (i + 1) % 4) for i in range(4)])
        behind = lax.ppermute(value, "op", [(i, (i + 3) % 4) for i in range(4)])
        far_a = lax.ppermute(ahead[:half], "op", [(i, (i + 1) % 4) for i in range(4)])
        far_b = lax.ppermute(behind[half:], "op", [(i, (i + 3) % 4) for i in range(4)])
        return [value, ahead, behind, far_a, far_b]

    stage = functools.partial(middle_stage, count, sizes)
    rows, cols = (left_dims, right_dims, starts[1]), (right_dims, left_dims, starts[0])
    chunks = left_stage(
        count, sizes, info, left_map[0], left_dims, right_dims, starts[0], wave.T, left_own
    )
    rights = over_op(right_own)
    arrived = exchange(chunks, 4 * count)
    left_late, arrived = lax.optimization_barrier((left_own, arrived))
    chunks = stage(False, False, info, maps[:, 1], *rows, arrived, rights)
    lefts = over_op(left_late)
    arrived = exchange(chunks, 4 * count)
    chunks = stage(True, False, info, maps[:, 0], *cols, arrived, lefts)
    arrived = exchange(chunks, 4 * count)
    piece = stage(True, True, info, maps[:, 1], *rows, arrived, rights)
    pieces = copies_to(piece, "op", 4)
    return pieces.reshape(4, 2, 8, count * 64).swapaxes(0, 1).reshape(64, count * 64)


def solution(mesh):
    n_op, n_sec = mesh.devices.shape
    ny = 4
    nz = n_sec // (2 * ny)
    split = Mesh(mesh.devices.reshape(n_op, nz, ny, 2), ALL)
    placed = (
        P(None, SEC),
        P("op", SEC, None, None),
        P("op", SEC, None, None),
        P("op", None),
        P("op", None),
        P(),
        P(),
    )
    return jax.shard_map(
        functools.partial(on_device, (nz, ny)),
        mesh=split, in_specs=placed, out_specs=P(SEC, None), check_vma=False,
    )
```

time: 358 us -> 357 us (level)
  waiting for transfers between devices: 100 us -> 74 us
  starting transfers between devices: 70.2 us -> 83.3 us
  Pallas kernels: 31.2 us -> 39.4 us
    all_to_all x2, waiting for transfers between devices: 46.4 us -> 2.28 us  [exchange(): return lax.all_to_all(pieces, ALL, 0, 0, tiled=True).reshape(shape)]
    ppermute x6 -> x8, waiting for transfers between devices: 53.9 us -> 71.7 us  [the longest x2 50.7 us: over_op(): behind = lax.ppermute(value, 'op', [(i, (i + 3) % 4) for i in range(4)])]
    ppermute x6 -> x8, starting transfers between devices: 20.1 us -> 28.2 us  [the longest x2 11.4 us: over_op(): lax.ppermute(behind[half:], 'op', [(i, (i + 3) % 4) for i in range(4)])]
    pallas_call x3, Pallas kernels: 26.4 us -> 33.7 us  [middle_stage(): pl.pallas_call(functools.partial(middle_kernel, count, sizes, turn, last)...]
    all_to_all x2, starting transfers between devices: 37.2 us -> 42.2 us  [exchange(): return lax.all_to_all(pieces, ALL, 0, 0, tiled=True).reshape(shape)]
    unnamed x29 -> x37, local copies, waits for them, and re-layouts: 11.2 us -> 12.5 us
  transfers between devices with their start and end apart: 10 -> 12, of which waited for: 5 -> 7; matrix products, arithmetic and copies ran while one was open for 1% -> 1% of each run, Pallas kernels for 1% -> 2%
where the time goes in v3:
time: 357 us; the launch traced here: 356 us
  blocking collectives  140 us (39%)
  starting transfers between devices  83.3 us (23%)
  waiting for transfers between devices  74 us (21%)
  Pallas kernels  39.4 us (11%)
  local copies, waits for them, and re-layouts  17.7 us (5%)
    all_to_all x1, blocking collectives, exchange(): return lax.all_to_all(pieces, ALL, 0, 0, tiled=True).reshape(shape)  79.6 us
    all_to_all x3, blocking collectives, copies_to(): lax.all_to_all(jnp.broadcast_to(value, (size,) + value.shape), axis, 0, 0...  60.8 us
    ppermute x2, waiting for transfers between devices, over_op(): behind = lax.ppermute(value, 'op', [(i, (i + 3) % 4) for i in range(4)])  50.7 us
    all_to_all x2, starting transfers between devices, exchange(): return lax.all_to_all(pieces, ALL, 0, 0, tiled=True).reshape(shape)  42.2 us
    pallas_call x3, Pallas kernels, middle_stage(): pl.pallas_call(functools.partial(middle_kernel, count, sizes, turn, last)...  33.7 us
    unnamed x37, local copies, waits for them, and re-layouts  12.5 us
    ppermute x2, starting transfers between devices, over_op(): lax.ppermute(behind[half:], 'op', [(i, (i + 3) % 4) for i in range(4)])  11.4 us
    ppermute x2, waiting for transfers between devices, over_op(): lax.ppermute(behind[half:], 'op', [(i, (i + 3) % 4) for i in range(4)])  10.7 us
  transfers between devices with their start and end apart: 12, of which 7 were waited for; matrix products, arithmetic and copies ran while one was open for 1% of the time, Pallas kernels for 2%

profile of v3, /device:TPU:1, one launch (start us, length us, event | category | flops | bytes accessed | tf_op | source)
XLA Modules:
  0.0 356.0 jit_solution(5496936578148258801)
XLA Ops:
  1.7 29.3 %all_to_all.35 = bf16[16,2,32,128]{3,2,1,0:T(8,128)(2,1)S(1)} all-to-all(bf16[16,2,32,128]{3,2,1,0:T(8,128)(2,1)S(1)} %broadcast_in_dim.13), channel_id=1, replica_groups=mesh['op'=4,'z'=16,'y'=4,'c'=2] {'z'}, dimensions={0} | all-to-all | bytes 524288 | tf_op jit(solution)/shard_map/all_to_all | solution.py:297
  31.2 13.7 %all_to_all.36 = bf16[4,16,2,32,128]{4,3,1,2,0:T(8,128)(2,1)S(1)} all-to-all(bf16[4,16,2,32,128]{4,3,1,2,0:T(8,128)(2,1)S(1)} %broadcast_in_dim.14), channel_id=1, replica_groups=mesh['op'=4,'z'=16,'y'=4,'c'=2] {'y'}, dimensions={0} | all-to-all | bytes 2097152 | tf_op jit(solution)/shard_map/all_to_all | solution.py:297
  46.0 8.9 %collective-permute-start = (bf16[4,16,2,32,128]{4,3,1,0,2:T(8,128)(2,1)}, bf16[4,16,2,32,128]{4,3,1,0,2:T(8,128)(2,1)S(1)}, u32[]{:S(2)}, u32[]{:S(2)}) collective-permute-start(bf16[4,16,2,32,128]{4,3,1,0,2:T(8,128)(2,1)} %copy.30), channel_id=1, source_target_pairs={{0,1},{1,0},{2,3},{3,2},{4,5},{5,4},{6,7},{7,6},{8,9},{9,8},{10,11... | collective-permute-start | bytes 3145736 | tf_op jit(solution)/shard_map/ppermute | solution.py:319
  55.5 4.0 %all-to-all-start = ((s32[4,2,128]{2,1,0:T(2,128)}), s32[4,2,128]{2,1,0:T(2,128)S(1)}, u32[]{:S(2)}, u32[]{:S(2)}) async-start(s32[4,2,128]{2,1,0:T(2,128)} %broadcast_in_dim.12), calls=%async_computation | async-start | bytes 8192 | tf_op jit(solution)/shard_map/all_to_all | solution.py:297
  62.1 5.7 %left_stage.1 = bf16[3072,128]{1,0:T(8,128)(2,1)} custom-call(s32[8]{0:T(128)S(1)} %stack.50.info, s32[128]{0:T(128)S(1)} %bitcast.65, s32[128]{0:T(128)S(1)} %copy-done.13, s32[128]{0:T(128)S(1)} %copy-done.14, s32[128]{0:T(128)S(1)} %sub.19.row_at.col_at, bf16[64,8192]{1,0:T(8,128)(2,1)S(1)} %bitcast.59, bf16[4096,128]{1,0:T(8,128)(2,1)S(1)} %bitcast.48), custom_call_target="tpu_custom_call" | custom-call | flops 134217728 | bytes 3145728 | tf_op jit(solution)/shard_map/left_stage/pallas_call | solution.py:254
  67.8 18.1 %all-to-all-start.3 = ((bf16[512,3,2,128]{3,2,1,0:T(2,128)(2,1)}), bf16[512,3,2,128]{3,2,1,0:T(2,128)(2,1)}, u32[]{:S(2)}, u32[]{:S(2)}) async-start(bf16[512,3,2,128]{3,2,1,0:T(2,128)(2,1)} %bitcast.23), calls=%async_computation.3 | async-start | bytes 1572864 | tf_op jit(solution)/shard_map/all_to_all | solution.py:303
  86.0 4.5 %collective-permute-start.2 = (bf16[4096,128]{1,0:T(8,128)(2,1)S(1)}, bf16[4096,128]{1,0:T(8,128)(2,1)S(1)}, u32[]{:S(2)}, u32[]{:S(2)}) collective-permute-start(bf16[4096,128]{1,0:T(8,128)(2,1)S(1)} %bitcast.52), channel_id=1, source_target_pairs={{0,384},{128,0},{256,128},{384,256},{1,385},{129,1},{257,129},{385... | collective-permute-start | bytes 3145736 | tf_op jit(solution)/shard_map/ppermute | solution.py:330
  92.5 25.3 %collective-permute-done.2.env_3 = bf16[4096,128]{1,0:T(8,128)(2,1)S(1)} collective-permute-done((bf16[4096,128]{1,0:T(8,128)(2,1)S(1)}, bf16[4096,128]{1,0:T(8,128)(2,1)S(1)}, u32[]{:S(2)}, u32[]{:S(2)}) %collective-permute-start.2) | collective-permute-done | bytes 1048608 | tf_op jit(solution)/shard_map/ppermute | solution.py:330
  118.6 5.7 %collective-permute-start.4 = (bf16[2048,128]{1,0:T(8,128)(2,1)}, bf16[2048,128]{1,0:T(8,128)(2,1)}, u32[]{:S(2)}, u32[]{:S(2)}) collective-permute-start(bf16[2048,128]{1,0:T(8,128)(2,1)} %slice.74), channel_id=1, source_target_pairs={{0,384},{128,0},{256,128},{384,256},{1,385},{129,1},{257,129},{385... | collective-permute-start | bytes 1572872 | tf_op jit(solution)/shard_map/ppermute | solution.py:332
  128.5 2.3 all-to-all-done.3
  130.7 3.4 collective-permute-done.4.env_2b
  134.1 6.4 %collective-permute-done.3.env_2a = bf16[2048,128]{1,0:T(8,128)(2,1)} collective-permute-done((bf16[2048,128]{1,0:T(8,128)(2,1)}, bf16[2048,128]{1,0:T(8,128)(2,1)}, u32[]{:S(2)}, u32[]{:S(2)}) %collective-permute-start.3) | collective-permute-done | bytes 524320 | tf_op jit(solution)/shard_map/ppermute | solution.py:331
  141.7 11.4 %middle_stage.2 = bf16[3072,128]{1,0:T(8,128)(2,1)S(1)} custom-call(s32[8]{0:T(128)S(1)} %stack.50.info, s32[4,128]{1,0:T(4,128)S(1)} %bitcast.60, s32[128]{0:T(128)S(1)} %copy-done.13, s32[128]{0:T(128)S(1)} %copy-done.14, s32[128]{0:T(128)S(1)} %sub.18.col_at, bf16[3072,128]{1,0:T(8,128)(2,1)} %bitcast.24.arrived, bf16[4096,128]{1,0:T(8,128)(2,1)S(1)} %bitcast.54, ...), custom_call_target="tpu_custom_call" | custom-call | flops 1073741824 | bytes 6291456 | tf_op jit(solution)/shard_map/middle_stage/pallas_call | solution.py:271
  154.1 24.1 %all-to-all-start.4 = ((bf16[512,3,2,128]{3,2,1,0:T(2,128)(2,1)}), bf16[512,3,2,128]{3,2,1,0:T(2,128)(2,1)}, u32[]{:S(2)}, u32[]{:S(2)}) async-start(bf16[512,3,2,128]{3,2,1,0:T(2,128)(2,1)} %bitcast.58), calls=%async_computation.4 | async-start | bytes 1572864 | tf_op jit(solution)/shard_map/all_to_all | solution.py:303
  178.1 4.5 %collective-permute-start.6 = (bf16[4096,128]{1,0:T(8,128)(2,1)S(1)}, bf16[4096,128]{1,0:T(8,128)(2,1)S(1)}, u32[]{:S(2)}, u32[]{:S(2)}) collective-permute-start(bf16[4096,128]{1,0:T(8,128)(2,1)S(1)} %bitcast.49), channel_id=1, source_target_pairs={{0,384},{128,0},{256,128},{384,256},{1,385},{129,1},{257,129},{385... | collective-permute-start | bytes 3145736 | tf_op jit(solution)/shard_map/ppermute | solution.py:330
  184.5 25.4 %collective-permute-done.6.env_3 = bf16[4096,128]{1,0:T(8,128)(2,1)S(1)} collective-permute-done((bf16[4096,128]{1,0:T(8,128)(2,1)S(1)}, bf16[4096,128]{1,0:T(8,128)(2,1)S(1)}, u32[]{:S(2)}, u32[]{:S(2)}) %collective-permute-start.6) | collective-permute-done | bytes 1048608 | tf_op jit(solution)/shard_map/ppermute | solution.py:330
  210.0 5.7 %collective-permute-start.8 = (bf16[2048,128]{1,0:T(8,128)(2,1)S(1)}, bf16[2048,128]{1,0:T(8,128)(2,1)S(1)}, u32[]{:S(2)}, u32[]{:S(2)}) collective-permute-start(bf16[2048,128]{1,0:T(8,128)(2,1)S(1)} %slice.76), channel_id=1, source_target_pairs={{0,384},{128,0},{256,128},{384,256},{1,385},{129,1},{257,129},{385... | collective-permute-start | bytes 1572872 | tf_op jit(solution)/shard_map/ppermute | solution.py:332
  215.8 2.1 collective-permute-start.7
  217.9 7.3 %collective-permute-done.8.env_2b = bf16[2048,128]{1,0:T(8,128)(2,1)S(1)} collective-permute-done((bf16[2048,128]{1,0:T(8,128)(2,1)S(1)}, bf16[2048,128]{1,0:T(8,128)(2,1)S(1)}, u32[]{:S(2)}, u32[]{:S(2)}) %collective-permute-start.8) | collective-permute-done | bytes 524320 | tf_op jit(solution)/shard_map/ppermute | solution.py:332
  226.0 3.8 %collective-permute-done.7.env_2a = bf16[2048,128]{1,0:T(8,128)(2,1)S(1)} collective-permute-done((bf16[2048,128]{1,0:T(8,128)(2,1)S(1)}, bf16[2048,128]{1,0:T(8,128)(2,1)S(1)}, u32[]{:S(2)}, u32[]{:S(2)}) %collective-permute-start.7) | collective-permute-done | bytes 524320 | tf_op jit(solution)/shard_map/ppermute | solution.py:331
  235.2 14.1 %middle_stage.3 = bf16[4096,128]{1,0:T(8,128)(2,1)S(1)} custom-call(s32[8]{0:T(128)S(1)} %stack.50.info, s32[4,128]{1,0:T(4,128)S(1)} %bitcast.64, s32[128]{0:T(128)S(1)} %copy-done.14, s32[128]{0:T(128)S(1)} %copy-done.13, s32[128]{0:T(128)S(1)} %sub.19.row_at.col_at, bf16[3072,128]{1,0:T(8,128)(2,1)} %bitcast.29.arrived, bf16[4096,128]{1,0:T(8,128)(2,1)S(1)} %bitcast.51, ...), custom_call_target="tpu_custom_call" | custom-call | flops 1073741824 | bytes 6291456 | tf_op jit(solution)/shard_map/middle_stage/pallas_call | solution.py:271
  249.4 79.6 %all_to_all.37 = bf16[512,4,2,128]{3,2,1,0:T(2,128)(2,1)S(1)} all-to-all(bf16[512,4,2,128]{3,2,1,0:T(2,128)(2,1)S(1)} %bitcast.56), channel_id=1, replica_groups=mesh['op'=4,'z'=16,'y'=4,'c'=2] {'op','z','y','c'}, dimensions={0} | all-to-all | bytes 2097152 | tf_op jit(solution)/shard_map/all_to_all | solution.py:303
  328.9 8.2 %last_stage.1 = bf16[16,8192]{1,0:T(8,128)(2,1)S(1)} custom-call(s32[8]{0:T(128)S(1)} %stack.50.info, s32[4,128]{1,0:T(4,128)S(1)} %bitcast.61, s32[128]{0:T(128)S(1)} %copy-done.13, s32[128]{0:T(128)S(1)} %copy-done.14, s32[128]{0:T(128)S(1)} %sub.18.col_at, bf16[4096,128]{1,0:T(8,128)(2,1)S(1)} %bitcast.57, bf16[4096,128]{1,0:T(8,128)(2,1)S(1)} %bitcast.55, ...), custom_call_target="tpu_custom_call" | custom-call | flops 1073741824 | bytes 6291456 | tf_op jit(solution)/shard_map/last_stage/pallas_call | solution.py:271
  337.2 17.8 %all_to_all.38 = bf16[4,16,8192]{2,1,0:T(8,128)(2,1)S(1)} all-to-all(bf16[4,16,8192]{2,1,0:T(8,128)(2,1)S(1)} %broadcast_in_dim.15), channel_id=1, replica_groups=mesh['op'=4,'z'=16,'y'=4,'c'=2] {'op'}, dimensions={0} | all-to-all | bytes 2097152 | tf_op jit(solution)/shard_map/all_to_all | solution.py:297
  (76 shorter events, 24.4 us)
Async XLA Ops:
  44.9 10.0 %copy-start.15 = (s32[1,128]{1,0:T(1,128)S(1)}, s32[1,128]{1,0:T(1,128)}, u32[]{:S(2)}) copy-start(s32[1,128]{1,0:T(1,128)} %param.10) | copy-start | bytes 1540
  44.9 10.0 %copy-start.17 = (s32[1,128]{1,0:T(1,128)S(1)}, s32[1,128]{1,0:T(1,128)}, u32[]{:S(2)}) copy-start(s32[1,128]{1,0:T(1,128)} %param.11) | copy-start | bytes 1540
  46.0 14.7 %collective-permute-start = (bf16[4,16,2,32,128]{4,3,1,0,2:T(8,128)(2,1)}, bf16[4,16,2,32,128]{4,3,1,0,2:T(8,128)(2,1)S(1)}, u32[]{:S(2)}, u32[]{:S(2)}) collective-permute-start(bf16[4,16,2,32,128]{4,3,1,0,2:T(8,128)(2,1)} %copy.30), channel_id=1, source_target_pairs={{0,1},{1,0},{2,3},{3,2},{4,5},{5,4},{6,7},{7,6},{8,9},{9,8},{10,11... | collective-permute-start | bytes 3145736 | tf_op jit(solution)/shard_map/ppermute | solution.py:319
  55.5 12.3 %all-to-all-start = ((s32[4,2,128]{2,1,0:T(2,128)}), s32[4,2,128]{2,1,0:T(2,128)S(1)}, u32[]{:S(2)}, u32[]{:S(2)}) async-start(s32[4,2,128]{2,1,0:T(2,128)} %broadcast_in_dim.12), calls=%async_computation | async-start | bytes 8192 | tf_op jit(solution)/shard_map/all_to_all | solution.py:297
  60.8 1.2 copy-start.8
  61.0 1.1 copy-start.14
  67.8 62.9 %all-to-all-start.3 = ((bf16[512,3,2,128]{3,2,1,0:T(2,128)(2,1)}), bf16[512,3,2,128]{3,2,1,0:T(2,128)(2,1)}, u32[]{:S(2)}, u32[]{:S(2)}) async-start(bf16[512,3,2,128]{3,2,1,0:T(2,128)(2,1)} %bitcast.23), calls=%async_computation.3 | async-start | bytes 1572864 | tf_op jit(solution)/shard_map/all_to_all | solution.py:303
  86.0 31.7 %collective-permute-start.2 = (bf16[4096,128]{1,0:T(8,128)(2,1)S(1)}, bf16[4096,128]{1,0:T(8,128)(2,1)S(1)}, u32[]{:S(2)}, u32[]{:S(2)}) collective-permute-start(bf16[4096,128]{1,0:T(8,128)(2,1)S(1)} %bitcast.52), channel_id=1, source_target_pairs={{0,384},{128,0},{256,128},{384,256},{1,385},{129,1},{257,129},{385... | collective-permute-start | bytes 3145736 | tf_op jit(solution)/shard_map/ppermute | solution.py:330
  90.5 33.8 %collective-permute-start.1 = (bf16[4096,128]{1,0:T(8,128)(2,1)S(1)}, bf16[4096,128]{1,0:T(8,128)(2,1)S(1)}, u32[]{:S(2)}, u32[]{:S(2)}) collective-permute-start(bf16[4096,128]{1,0:T(8,128)(2,1)S(1)} %bitcast.53), channel_id=1, source_target_pairs={{0,128},{128,256},{256,384},{384,0},{1,129},{129,257},{257,385},{3... | collective-permute-start | bytes 3145736 | tf_op jit(solution)/shard_map/ppermute | solution.py:329
  118.6 15.5 %collective-permute-start.4 = (bf16[2048,128]{1,0:T(8,128)(2,1)}, bf16[2048,128]{1,0:T(8,128)(2,1)}, u32[]{:S(2)}, u32[]{:S(2)}) collective-permute-start(bf16[2048,128]{1,0:T(8,128)(2,1)} %slice.74), channel_id=1, source_target_pairs={{0,384},{128,0},{256,128},{384,256},{1,385},{129,1},{257,129},{385... | collective-permute-start | bytes 1572872 | tf_op jit(solution)/shard_map/ppermute | solution.py:332
  126.1 14.4 %collective-permute-start.3 = (bf16[2048,128]{1,0:T(8,128)(2,1)}, bf16[2048,128]{1,0:T(8,128)(2,1)}, u32[]{:S(2)}, u32[]{:S(2)}) collective-permute-start(bf16[2048,128]{1,0:T(8,128)(2,1)} %slice.73), channel_id=1, source_target_pairs={{0,128},{128,256},{256,384},{384,0},{1,129},{129,257},{257,385},{3... | collective-permute-start | bytes 1572872 | tf_op jit(solution)/shard_map/ppermute | solution.py:331
  140.5 1.2 copy-start.1
  154.1 76.6 %all-to-all-start.4 = ((bf16[512,3,2,128]{3,2,1,0:T(2,128)(2,1)}), bf16[512,3,2,128]{3,2,1,0:T(2,128)(2,1)}, u32[]{:S(2)}, u32[]{:S(2)}) async-start(bf16[512,3,2,128]{3,2,1,0:T(2,128)(2,1)} %bitcast.58), calls=%async_computation.4 | async-start | bytes 1572864 | tf_op jit(solution)/shard_map/all_to_all | solution.py:303
  178.1 31.8 %collective-permute-start.6 = (bf16[4096,128]{1,0:T(8,128)(2,1)S(1)}, bf16[4096,128]{1,0:T(8,128)(2,1)S(1)}, u32[]{:S(2)}, u32[]{:S(2)}) collective-permute-start(bf16[4096,128]{1,0:T(8,128)(2,1)S(1)} %bitcast.49), channel_id=1, source_target_pairs={{0,384},{128,0},{256,128},{384,256},{1,385},{129,1},{257,129},{385... | collective-permute-start | bytes 3145736 | tf_op jit(solution)/shard_map/ppermute | solution.py:330
  182.6 33.1 %collective-permute-start.5 = (bf16[4096,128]{1,0:T(8,128)(2,1)S(1)}, bf16[4096,128]{1,0:T(8,128)(2,1)S(1)}, u32[]{:S(2)}, u32[]{:S(2)}) collective-permute-start(bf16[4096,128]{1,0:T(8,128)(2,1)S(1)} %bitcast.50), channel_id=1, source_target_pairs={{0,128},{128,256},{256,384},{384,0},{1,129},{129,257},{257,385},{3... | collective-permute-start | bytes 3145736 | tf_op jit(solution)/shard_map/ppermute | solution.py:329
  209.9 5.8 %copy-start.4 = (bf16[4096,128]{1,0:T(8,128)(2,1)}, bf16[4096,128]{1,0:T(8,128)(2,1)S(1)}, u32[]{:S(2)}) copy-start(bf16[4096,128]{1,0:T(8,128)(2,1)S(1)} %collective-permute-done.6.env_3) | copy-start | bytes 3145732
  210.0 15.3 %collective-permute-start.8 = (bf16[2048,128]{1,0:T(8,128)(2,1)S(1)}, bf16[2048,128]{1,0:T(8,128)(2,1)S(1)}, u32[]{:S(2)}, u32[]{:S(2)}) collective-permute-start(bf16[2048,128]{1,0:T(8,128)(2,1)S(1)} %slice.76), channel_id=1, source_target_pairs={{0,384},{128,0},{256,128},{384,256},{1,385},{129,1},{257,129},{385... | collective-permute-start | bytes 1572872 | tf_op jit(solution)/shard_map/ppermute | solution.py:332
  215.7 2.2 copy-start.6
  215.8 14.1 %collective-permute-start.7 = (bf16[2048,128]{1,0:T(8,128)(2,1)S(1)}, bf16[2048,128]{1,0:T(8,128)(2,1)S(1)}, u32[]{:S(2)}, u32[]{:S(2)}) collective-permute-start(bf16[2048,128]{1,0:T(8,128)(2,1)S(1)} %slice.75), channel_id=1, source_target_pairs={{0,128},{128,256},{256,384},{384,0},{1,129},{129,257},{257,385},{3... | collective-permute-start | bytes 1572872 | tf_op jit(solution)/shard_map/ppermute | solution.py:331
  230.7 1.2 copy-start.5
  231.9 1.2 copy-start.7
  233.1 1.0 copy-start.10
  234.2 1.0 copy-start.12
  249.4 79.6 %copy-start.2 = (bf16[4096,128]{1,0:T(8,128)(2,1)S(1)}, bf16[4096,128]{1,0:T(8,128)(2,1)}, u32[]{:S(2)}) copy-start(bf16[4096,128]{1,0:T(8,128)(2,1)} %copy-done) | copy-start | bytes 3145732
  (6 other events, 4.9 us)

commit v4 on v3

--- a/solution.py
+++ b/solution.py
@@ -7,6 +7,7 @@
 from jax.experimental.pallas import tpu as pltpu
 from jax.sharding import Mesh
 from jax.sharding import PartitionSpec as P
+
 
 BF16, F32 = jnp.bfloat16, jnp.float32
 NT = (((1,), (1,)), ((), ()))
@@ -303,7 +304,7 @@
     return lax.all_to_all(pieces, ALL, 0, 0, tiled=True).reshape(shape)
 
 
-def on_device(sizes, wave, left_env, right_env, left_map, right_map, left_dims, right_dims):
+def program(sizes, wave, left_env, right_env, left_map, right_map, left_dims, right_dims):
     nz, ny = sizes
     count = left_map.shape[1]
     me, core = lax.axis_index("op"), lax.axis_index("c")
@@ -334,14 +335,13 @@
 
     stage = functools.partial(middle_stage, count, sizes)
     rows, cols = (left_dims, right_dims, starts[1]), (right_dims, left_dims, starts[0])
+    rights = over_op(right_own)
+    lefts = over_op(left_own)
     chunks = left_stage(
         count, sizes, info, left_map[0], left_dims, right_dims, starts[0], wave.T, left_own
     )
-    rights = over_op(right_own)
     arrived = exchange(chunks, 4 * count)
-    left_late, arrived = lax.optimization_barrier((left_own, arrived))
     chunks = stage(False, False, info, maps[:, 1], *rows, arrived, rights)
-    lefts = over_op(left_late)
     arrived = exchange(chunks, 4 * count)
     chunks = stage(True, False, info, maps[:, 0], *cols, arrived, lefts)
     arrived = exchange(chunks, 4 * count)
@@ -365,6 +365,6 @@
         P(),
     )
     return jax.shard_map(
-        functools.partial(on_device, (nz, ny)),
+        functools.partial(program, (nz, ny)),
         mesh=split, in_specs=placed, out_specs=P(SEC, None), check_vma=False,
     )

time: 357 us -> 357 us (level)
  transfers between devices with their start and end apart: 12 -> 12, of which waited for: 7 -> 6; matrix products, arithmetic and copies ran while one was open for 1% -> 1% of each run, Pallas kernels for 2% -> 2%
where the time goes in v4:
time: 357 us; the launch traced here: 356 us
  blocking collectives  140 us (39%)
  starting transfers between devices  83.3 us (23%)
  waiting for transfers between devices  73.9 us (21%)
  Pallas kernels  39.4 us (11%)
  local copies, waits for them, and re-layouts  17.7 us (5%)
    all_to_all x1, blocking collectives, exchange(): return lax.all_to_all(pieces, ALL, 0, 0, tiled=True).reshape(shape)  79.6 us
    all_to_all x3, blocking collectives, copies_to(): lax.all_to_all(jnp.broadcast_to(value, (size,) + value.shape), axis, 0, 0...  60.8 us
    ppermute x2, waiting for transfers between devices, over_op(): behind = lax.ppermute(value, 'op', [(i, (i + 3) % 4) for i in range(4)])  50.7 us
    all_to_all x2, starting transfers between devices, exchange(): return lax.all_to_all(pieces, ALL, 0, 0, tiled=True).reshape(shape)  42.2 us
    pallas_call x3, Pallas kernels, middle_stage(): pl.pallas_call(functools.partial(middle_kernel, count, sizes, turn, last)...  33.7 us
    ppermute x2, waiting for transfers between devices, over_op(): lax.ppermute(behind[half:], 'op', [(i, (i + 3) % 4) for i in range(4)])  13 us
    unnamed x37, local copies, waits for them, and re-layouts  12.5 us
    ppermute x2, starting transfers between devices, over_op(): lax.ppermute(behind[half:], 'op', [(i, (i + 3) % 4) for i in range(4)])  11.4 us
  transfers between devices with their start and end apart: 12, of which 6 were waited for; matrix products, arithmetic and copies ran while one was open for 1% of the time, Pallas kernels for 2%

profile of v4, /device:TPU:1, one launch (start us, length us, event | category | flops | bytes accessed | tf_op | source)
XLA Modules:
  0.0 355.9 jit_solution(12540500802347605483)
XLA Ops:
  1.7 29.3 %all_to_all.35 = bf16[16,2,32,128]{3,2,1,0:T(8,128)(2,1)S(1)} all-to-all(bf16[16,2,32,128]{3,2,1,0:T(8,128)(2,1)S(1)} %broadcast_in_dim.13), channel_id=1, replica_groups=mesh['op'=4,'z'=16,'y'=4,'c'=2] {'z'}, dimensions={0} | all-to-all | bytes 524288 | tf_op jit(solution)/shard_map/all_to_all | solution.py:298
  31.2 13.7 %all_to_all.36 = bf16[4,16,2,32,128]{4,3,1,2,0:T(8,128)(2,1)S(1)} all-to-all(bf16[4,16,2,32,128]{4,3,1,2,0:T(8,128)(2,1)S(1)} %broadcast_in_dim.14), channel_id=1, replica_groups=mesh['op'=4,'z'=16,'y'=4,'c'=2] {'y'}, dimensions={0} | all-to-all | bytes 2097152 | tf_op jit(solution)/shard_map/all_to_all | solution.py:298
  46.0 8.9 %collective-permute-start = (bf16[4,16,2,32,128]{4,3,1,0,2:T(8,128)(2,1)}, bf16[4,16,2,32,128]{4,3,1,0,2:T(8,128)(2,1)S(1)}, u32[]{:S(2)}, u32[]{:S(2)}) collective-permute-start(bf16[4,16,2,32,128]{4,3,1,0,2:T(8,128)(2,1)} %copy.30), channel_id=1, source_target_pairs={{0,1},{1,0},{2,3},{3,2},{4,5},{5,4},{6,7},{7,6},{8,9},{9,8},{10,11... | collective-permute-start | bytes 3145736 | tf_op jit(solution)/shard_map/ppermute | solution.py:320
  55.5 4.0 %all-to-all-start = ((s32[4,2,128]{2,1,0:T(2,128)}), s32[4,2,128]{2,1,0:T(2,128)S(1)}, u32[]{:S(2)}, u32[]{:S(2)}) async-start(s32[4,2,128]{2,1,0:T(2,128)} %broadcast_in_dim.12), calls=%async_computation | async-start | bytes 8192 | tf_op jit(solution)/shard_map/all_to_all | solution.py:298
  62.1 5.7 %left_stage.1 = bf16[3072,128]{1,0:T(8,128)(2,1)} custom-call(s32[8]{0:T(128)S(1)} %stack.50.info, s32[128]{0:T(128)S(1)} %bitcast.65, s32[128]{0:T(128)S(1)} %copy-done.13, s32[128]{0:T(128)S(1)} %copy-done.14, s32[128]{0:T(128)S(1)} %sub.19.row_at.col_at, bf16[64,8192]{1,0:T(8,128)(2,1)S(1)} %bitcast.59, bf16[4096,128]{1,0:T(8,128)(2,1)S(1)} %bitcast.48), custom_call_target="tpu_custom_call" | custom-call | flops 134217728 | bytes 3145728 | tf_op jit(solution)/shard_map/left_stage/pallas_call | solution.py:255
  67.7 18.1 %all-to-all-start.3 = ((bf16[512,3,2,128]{3,2,1,0:T(2,128)(2,1)}), bf16[512,3,2,128]{3,2,1,0:T(2,128)(2,1)}, u32[]{:S(2)}, u32[]{:S(2)}) async-start(bf16[512,3,2,128]{3,2,1,0:T(2,128)(2,1)} %bitcast.23), calls=%async_computation.3 | async-start | bytes 1572864 | tf_op jit(solution)/shard_map/all_to_all | solution.py:304
  86.0 4.5 %collective-permute-start.2 = (bf16[4096,128]{1,0:T(8,128)(2,1)S(1)}, bf16[4096,128]{1,0:T(8,128)(2,1)S(1)}, u32[]{:S(2)}, u32[]{:S(2)}) collective-permute-start(bf16[4096,128]{1,0:T(8,128)(2,1)S(1)} %bitcast.52), channel_id=1, source_target_pairs={{0,384},{128,0},{256,128},{384,256},{1,385},{129,1},{257,129},{385... | collective-permute-start | bytes 3145736 | tf_op jit(solution)/shard_map/ppermute | solution.py:331
  90.5 1.9 collective-permute-start.1
  92.4 25.3 %collective-permute-done.2.env_3 = bf16[4096,128]{1,0:T(8,128)(2,1)S(1)} collective-permute-done((bf16[4096,128]{1,0:T(8,128)(2,1)S(1)}, bf16[4096,128]{1,0:T(8,128)(2,1)S(1)}, u32[]{:S(2)}, u32[]{:S(2)}) %collective-permute-start.2) | collective-permute-done | bytes 1048608 | tf_op jit(solution)/shard_map/ppermute | solution.py:331
  118.5 5.7 %collective-permute-start.4 = (bf16[2048,128]{1,0:T(8,128)(2,1)}, bf16[2048,128]{1,0:T(8,128)(2,1)}, u32[]{:S(2)}, u32[]{:S(2)}) collective-permute-start(bf16[2048,128]{1,0:T(8,128)(2,1)} %slice.74), channel_id=1, source_target_pairs={{0,384},{128,0},{256,128},{384,256},{1,385},{129,1},{257,129},{385... | collective-permute-start | bytes 1572872 | tf_op jit(solution)/shard_map/ppermute | solution.py:333
  128.4 5.7 %collective-permute-done.4.env_2b = bf16[2048,128]{1,0:T(8,128)(2,1)} collective-permute-done((bf16[2048,128]{1,0:T(8,128)(2,1)}, bf16[2048,128]{1,0:T(8,128)(2,1)}, u32[]{:S(2)}, u32[]{:S(2)}) %collective-permute-start.4) | collective-permute-done | bytes 524320 | tf_op jit(solution)/shard_map/ppermute | solution.py:333
  134.1 6.4 %collective-permute-done.3.env_2a = bf16[2048,128]{1,0:T(8,128)(2,1)} collective-permute-done((bf16[2048,128]{1,0:T(8,128)(2,1)}, bf16[2048,128]{1,0:T(8,128)(2,1)}, u32[]{:S(2)}, u32[]{:S(2)}) %collective-permute-start.3) | collective-permute-done | bytes 524320 | tf_op jit(solution)/shard_map/ppermute | solution.py:332
  141.7 11.4 %middle_stage.2 = bf16[3072,128]{1,0:T(8,128)(2,1)S(1)} custom-call(s32[8]{0:T(128)S(1)} %stack.50.info, s32[4,128]{1,0:T(4,128)S(1)} %bitcast.60, s32[128]{0:T(128)S(1)} %copy-done.13, s32[128]{0:T(128)S(1)} %copy-done.14, s32[128]{0:T(128)S(1)} %sub.18.col_at, bf16[3072,128]{1,0:T(8,128)(2,1)} %bitcast.24.arrived, bf16[4096,128]{1,0:T(8,128)(2,1)S(1)} %bitcast.54, ...), custom_call_target="tpu_custom_call" | custom-call | flops 1073741824 | bytes 6291456 | tf_op jit(solution)/shard_map/middle_stage/pallas_call | solution.py:272
  154.0 24.1 %all-to-all-start.4 = ((bf16[512,3,2,128]{3,2,1,0:T(2,128)(2,1)}), bf16[512,3,2,128]{3,2,1,0:T(2,128)(2,1)}, u32[]{:S(2)}, u32[]{:S(2)}) async-start(bf16[512,3,2,128]{3,2,1,0:T(2,128)(2,1)} %bitcast.58), calls=%async_computation.4 | async-start | bytes 1572864 | tf_op jit(solution)/shard_map/all_to_all | solution.py:304
  178.1 4.5 %collective-permute-start.6 = (bf16[4096,128]{1,0:T(8,128)(2,1)S(1)}, bf16[4096,128]{1,0:T(8,128)(2,1)S(1)}, u32[]{:S(2)}, u32[]{:S(2)}) collective-permute-start(bf16[4096,128]{1,0:T(8,128)(2,1)S(1)} %bitcast.49), channel_id=1, source_target_pairs={{0,384},{128,0},{256,128},{384,256},{1,385},{129,1},{257,129},{385... | collective-permute-start | bytes 3145736 | tf_op jit(solution)/shard_map/ppermute | solution.py:331
  184.5 25.4 %collective-permute-done.6.env_3 = bf16[4096,128]{1,0:T(8,128)(2,1)S(1)} collective-permute-done((bf16[4096,128]{1,0:T(8,128)(2,1)S(1)}, bf16[4096,128]{1,0:T(8,128)(2,1)S(1)}, u32[]{:S(2)}, u32[]{:S(2)}) %collective-permute-start.6) | collective-permute-done | bytes 1048608 | tf_op jit(solution)/shard_map/ppermute | solution.py:331
  209.9 5.7 %collective-permute-start.8 = (bf16[2048,128]{1,0:T(8,128)(2,1)S(1)}, bf16[2048,128]{1,0:T(8,128)(2,1)S(1)}, u32[]{:S(2)}, u32[]{:S(2)}) collective-permute-start(bf16[2048,128]{1,0:T(8,128)(2,1)S(1)} %slice.76), channel_id=1, source_target_pairs={{0,384},{128,0},{256,128},{384,256},{1,385},{129,1},{257,129},{385... | collective-permute-start | bytes 1572872 | tf_op jit(solution)/shard_map/ppermute | solution.py:333
  215.7 2.1 collective-permute-start.7
  217.8 7.3 %collective-permute-done.8.env_2b = bf16[2048,128]{1,0:T(8,128)(2,1)S(1)} collective-permute-done((bf16[2048,128]{1,0:T(8,128)(2,1)S(1)}, bf16[2048,128]{1,0:T(8,128)(2,1)S(1)}, u32[]{:S(2)}, u32[]{:S(2)}) %collective-permute-start.8) | collective-permute-done | bytes 524320 | tf_op jit(solution)/shard_map/ppermute | solution.py:333
  226.0 3.8 %collective-permute-done.7.env_2a = bf16[2048,128]{1,0:T(8,128)(2,1)S(1)} collective-permute-done((bf16[2048,128]{1,0:T(8,128)(2,1)S(1)}, bf16[2048,128]{1,0:T(8,128)(2,1)S(1)}, u32[]{:S(2)}, u32[]{:S(2)}) %collective-permute-start.7) | collective-permute-done | bytes 524320 | tf_op jit(solution)/shard_map/ppermute | solution.py:332
  235.2 14.1 %middle_stage.3 = bf16[4096,128]{1,0:T(8,128)(2,1)S(1)} custom-call(s32[8]{0:T(128)S(1)} %stack.50.info, s32[4,128]{1,0:T(4,128)S(1)} %bitcast.64, s32[128]{0:T(128)S(1)} %copy-done.14, s32[128]{0:T(128)S(1)} %copy-done.13, s32[128]{0:T(128)S(1)} %sub.19.row_at.col_at, bf16[3072,128]{1,0:T(8,128)(2,1)} %bitcast.29.arrived, bf16[4096,128]{1,0:T(8,128)(2,1)S(1)} %bitcast.51, ...), custom_call_target="tpu_custom_call" | custom-call | flops 1073741824 | bytes 6291456 | tf_op jit(solution)/shard_map/middle_stage/pallas_call | solution.py:272
  249.3 79.6 %all_to_all.37 = bf16[512,4,2,128]{3,2,1,0:T(2,128)(2,1)S(1)} all-to-all(bf16[512,4,2,128]{3,2,1,0:T(2,128)(2,1)S(1)} %bitcast.56), channel_id=1, replica_groups=mesh['op'=4,'z'=16,'y'=4,'c'=2] {'op','z','y','c'}, dimensions={0} | all-to-all | bytes 2097152 | tf_op jit(solution)/shard_map/all_to_all | solution.py:304
  328.9 8.1 %last_stage.1 = bf16[16,8192]{1,0:T(8,128)(2,1)S(1)} custom-call(s32[8]{0:T(128)S(1)} %stack.50.info, s32[4,128]{1,0:T(4,128)S(1)} %bitcast.61, s32[128]{0:T(128)S(1)} %copy-done.13, s32[128]{0:T(128)S(1)} %copy-done.14, s32[128]{0:T(128)S(1)} %sub.18.col_at, bf16[4096,128]{1,0:T(8,128)(2,1)S(1)} %bitcast.57, bf16[4096,128]{1,0:T(8,128)(2,1)S(1)} %bitcast.55, ...), custom_call_target="tpu_custom_call" | custom-call | flops 1073741824 | bytes 6291456 | tf_op jit(solution)/shard_map/last_stage/pallas_call | solution.py:272
  337.1 17.8 %all_to_all.38 = bf16[4,16,8192]{2,1,0:T(8,128)(2,1)S(1)} all-to-all(bf16[4,16,8192]{2,1,0:T(8,128)(2,1)S(1)} %broadcast_in_dim.15), channel_id=1, replica_groups=mesh['op'=4,'z'=16,'y'=4,'c'=2] {'op'}, dimensions={0} | all-to-all | bytes 2097152 | tf_op jit(solution)/shard_map/all_to_all | solution.py:298
  (76 shorter events, 22.4 us)
Async XLA Ops:
  44.9 10.0 %copy-start.15 = (s32[1,128]{1,0:T(1,128)S(1)}, s32[1,128]{1,0:T(1,128)}, u32[]{:S(2)}) copy-start(s32[1,128]{1,0:T(1,128)} %param.10) | copy-start | bytes 1540
  44.9 10.0 %copy-start.17 = (s32[1,128]{1,0:T(1,128)S(1)}, s32[1,128]{1,0:T(1,128)}, u32[]{:S(2)}) copy-start(s32[1,128]{1,0:T(1,128)} %param.11) | copy-start | bytes 1540
  46.0 14.7 %collective-permute-start = (bf16[4,16,2,32,128]{4,3,1,0,2:T(8,128)(2,1)}, bf16[4,16,2,32,128]{4,3,1,0,2:T(8,128)(2,1)S(1)}, u32[]{:S(2)}, u32[]{:S(2)}) collective-permute-start(bf16[4,16,2,32,128]{4,3,1,0,2:T(8,128)(2,1)} %copy.30), channel_id=1, source_target_pairs={{0,1},{1,0},{2,3},{3,2},{4,5},{5,4},{6,7},{7,6},{8,9},{9,8},{10,11... | collective-permute-start | bytes 3145736 | tf_op jit(solution)/shard_map/ppermute | solution.py:320
  55.5 12.2 %all-to-all-start = ((s32[4,2,128]{2,1,0:T(2,128)}), s32[4,2,128]{2,1,0:T(2,128)S(1)}, u32[]{:S(2)}, u32[]{:S(2)}) async-start(s32[4,2,128]{2,1,0:T(2,128)} %broadcast_in_dim.12), calls=%async_computation | async-start | bytes 8192 | tf_op jit(solution)/shard_map/all_to_all | solution.py:298
  60.8 1.2 copy-start.8
  60.9 1.1 copy-start.14
  67.7 72.7 %all-to-all-start.3 = ((bf16[512,3,2,128]{3,2,1,0:T(2,128)(2,1)}), bf16[512,3,2,128]{3,2,1,0:T(2,128)(2,1)}, u32[]{:S(2)}, u32[]{:S(2)}) async-start(bf16[512,3,2,128]{3,2,1,0:T(2,128)(2,1)} %bitcast.23), calls=%async_computation.3 | async-start | bytes 1572864 | tf_op jit(solution)/shard_map/all_to_all | solution.py:304
  86.0 31.7 %collective-permute-start.2 = (bf16[4096,128]{1,0:T(8,128)(2,1)S(1)}, bf16[4096,128]{1,0:T(8,128)(2,1)S(1)}, u32[]{:S(2)}, u32[]{:S(2)}) collective-permute-start(bf16[4096,128]{1,0:T(8,128)(2,1)S(1)} %bitcast.52), channel_id=1, source_target_pairs={{0,384},{128,0},{256,128},{384,256},{1,385},{129,1},{257,129},{385... | collective-permute-start | bytes 3145736 | tf_op jit(solution)/shard_map/ppermute | solution.py:331
  90.5 33.8 %collective-permute-start.1 = (bf16[4096,128]{1,0:T(8,128)(2,1)S(1)}, bf16[4096,128]{1,0:T(8,128)(2,1)S(1)}, u32[]{:S(2)}, u32[]{:S(2)}) collective-permute-start(bf16[4096,128]{1,0:T(8,128)(2,1)S(1)} %bitcast.53), channel_id=1, source_target_pairs={{0,128},{128,256},{256,384},{384,0},{1,129},{129,257},{257,385},{3... | collective-permute-start | bytes 3145736 | tf_op jit(solution)/shard_map/ppermute | solution.py:330
  118.5 15.5 %collective-permute-start.4 = (bf16[2048,128]{1,0:T(8,128)(2,1)}, bf16[2048,128]{1,0:T(8,128)(2,1)}, u32[]{:S(2)}, u32[]{:S(2)}) collective-permute-start(bf16[2048,128]{1,0:T(8,128)(2,1)} %slice.74), channel_id=1, source_target_pairs={{0,384},{128,0},{256,128},{384,256},{1,385},{129,1},{257,129},{385... | collective-permute-start | bytes 1572872 | tf_op jit(solution)/shard_map/ppermute | solution.py:333
  126.1 14.4 %collective-permute-start.3 = (bf16[2048,128]{1,0:T(8,128)(2,1)}, bf16[2048,128]{1,0:T(8,128)(2,1)}, u32[]{:S(2)}, u32[]{:S(2)}) collective-permute-start(bf16[2048,128]{1,0:T(8,128)(2,1)} %slice.73), channel_id=1, source_target_pairs={{0,128},{128,256},{256,384},{384,0},{1,129},{129,257},{257,385},{3... | collective-permute-start | bytes 1572872 | tf_op jit(solution)/shard_map/ppermute | solution.py:332
  140.4 1.2 copy-start.1
  154.0 76.6 %all-to-all-start.4 = ((bf16[512,3,2,128]{3,2,1,0:T(2,128)(2,1)}), bf16[512,3,2,128]{3,2,1,0:T(2,128)(2,1)}, u32[]{:S(2)}, u32[]{:S(2)}) async-start(bf16[512,3,2,128]{3,2,1,0:T(2,128)(2,1)} %bitcast.58), calls=%async_computation.4 | async-start | bytes 1572864 | tf_op jit(solution)/shard_map/all_to_all | solution.py:304
  178.1 31.8 %collective-permute-start.6 = (bf16[4096,128]{1,0:T(8,128)(2,1)S(1)}, bf16[4096,128]{1,0:T(8,128)(2,1)S(1)}, u32[]{:S(2)}, u32[]{:S(2)}) collective-permute-start(bf16[4096,128]{1,0:T(8,128)(2,1)S(1)} %bitcast.49), channel_id=1, source_target_pairs={{0,384},{128,0},{256,128},{384,256},{1,385},{129,1},{257,129},{385... | collective-permute-start | bytes 3145736 | tf_op jit(solution)/shard_map/ppermute | solution.py:331
  182.6 33.1 %collective-permute-start.5 = (bf16[4096,128]{1,0:T(8,128)(2,1)S(1)}, bf16[4096,128]{1,0:T(8,128)(2,1)S(1)}, u32[]{:S(2)}, u32[]{:S(2)}) collective-permute-start(bf16[4096,128]{1,0:T(8,128)(2,1)S(1)} %bitcast.50), channel_id=1, source_target_pairs={{0,128},{128,256},{256,384},{384,0},{1,129},{129,257},{257,385},{3... | collective-permute-start | bytes 3145736 | tf_op jit(solution)/shard_map/ppermute | solution.py:330
  209.9 5.8 %copy-start.4 = (bf16[4096,128]{1,0:T(8,128)(2,1)}, bf16[4096,128]{1,0:T(8,128)(2,1)S(1)}, u32[]{:S(2)}) copy-start(bf16[4096,128]{1,0:T(8,128)(2,1)S(1)} %collective-permute-done.6.env_3) | copy-start | bytes 3145732
  209.9 15.3 %collective-permute-start.8 = (bf16[2048,128]{1,0:T(8,128)(2,1)S(1)}, bf16[2048,128]{1,0:T(8,128)(2,1)S(1)}, u32[]{:S(2)}, u32[]{:S(2)}) collective-permute-start(bf16[2048,128]{1,0:T(8,128)(2,1)S(1)} %slice.76), channel_id=1, source_target_pairs={{0,384},{128,0},{256,128},{384,256},{1,385},{129,1},{257,129},{385... | collective-permute-start | bytes 1572872 | tf_op jit(solution)/shard_map/ppermute | solution.py:333
  215.6 2.2 copy-start.6
  215.7 14.1 %collective-permute-start.7 = (bf16[2048,128]{1,0:T(8,128)(2,1)S(1)}, bf16[2048,128]{1,0:T(8,128)(2,1)S(1)}, u32[]{:S(2)}, u32[]{:S(2)}) collective-permute-start(bf16[2048,128]{1,0:T(8,128)(2,1)S(1)} %slice.75), channel_id=1, source_target_pairs={{0,128},{128,256},{256,384},{384,0},{1,129},{129,257},{257,385},{3... | collective-permute-start | bytes 1572872 | tf_op jit(solution)/shard_map/ppermute | solution.py:332
  230.6 1.2 copy-start.5
  231.8 1.2 copy-start.7
  233.1 1.0 copy-start.10
  234.1 1.0 copy-start.12
  249.3 79.6 %copy-start.2 = (bf16[4096,128]{1,0:T(8,128)(2,1)S(1)}, bf16[4096,128]{1,0:T(8,128)(2,1)}, u32[]{:S(2)}) copy-start(bf16[4096,128]{1,0:T(8,128)(2,1)} %copy-done) | copy-start | bytes 3145732
  (6 other events, 4.9 us)

commit v5 on v4

--- a/solution.py
+++ b/solution.py
@@ -189,7 +189,7 @@
     def summed(block):
         lhs = []
         for w in range(4):
-            t = tiles[w, source[w, block]]
+            t = tiles[w, source[(info[0] - w) & 3, block]]
             lhs.append(jnp.concatenate([jnp.where(low, t, zero), jnp.where(low, zero, t)], axis=0))
         lhs = jnp.concatenate(lhs, axis=1)
         total = lax.dot_general(lhs, env_of(block), NT, preferred_element_type=F32)
@@ -218,7 +218,7 @@
     def product(block):
         slots = []
         for w in range(4):
-            both = held[source[w, block]]
+            both = held[source[(info[0] - w) & 3, block]]
             rows = []
             for h in range(2):
                 tile = jnp.where(low, both, zero) if h == 0 else jnp.where(low, zero, both)
@@ -313,7 +313,6 @@
     starts = [jnp.cumsum(d) - d for d in (left_dims, right_dims)]
     info = jnp.stack([me, sector, core] + [lax.rem(me + 4 - s, 4) for s in shifts] + [me]).astype(jnp.int32)
 
-    maps = copies_to(jnp.stack([left_map[0], right_map[0]]), "op", 4)
     own = jnp.stack([fold(left_env[0, 0]), fold(right_env[0, 0].T)])
     over_z = copies_to(own, "z", nz)
     over_y = copies_to(over_z, "y", ny)
@@ -340,6 +339,9 @@
     chunks = left_stage(
         count, sizes, info, left_map[0], left_dims, right_dims, starts[0], wave.T, left_own
     )
+    own_maps, chunks = lax.optimization_barrier((jnp.stack([left_map[0], right_map[0]]), chunks))
+    others = [lax.ppermute(own_maps, "op", [(i, (i + k) % 4) for i in range(4)]) for k in (1, 2, 3)]
+    maps = jnp.stack([own_maps] + others)
     arrived = exchange(chunks, 4 * count)
     chunks = stage(False, False, info, maps[:, 1], *rows, arrived, rights)
     arrived = exchange(chunks, 4 * count)

time: 357 us -> 356 us (level)
  waiting for transfers between devices: 73.9 us -> 65.7 us
  starting transfers between devices: 83.3 us -> 88.9 us
    ppermute x0 -> x3, starting transfers between devices: none -> 8.98 us  [program(): lax.ppermute(own_maps, 'op', [(i, (i + k) % 4) for i in range(4)])]
    ppermute x2, waiting for transfers between devices: 10.2 us -> 3.81 us  [over_op(): lax.ppermute(ahead[:half], 'op', [(i, (i + 1) % 4) for i in range(4)])]
    ppermute x2, waiting for transfers between devices: 13 us -> 7.39 us  [over_op(): lax.ppermute(behind[half:], 'op', [(i, (i + 3) % 4) for i in range(4)])]
    all_to_all x1 -> x0, starting transfers between devices: 4.01 us -> none  [copies_to(): lax.all_to_all(jnp.broadcast_to(value, (size,) + value.shape), axis, 0, 0...]
  transfers between devices with their start and end apart: 12 -> 14, of which waited for: 6 -> 7; matrix products, arithmetic and copies ran while one was open for 1% -> 1% of each run, Pallas kernels for 2% -> 0%
where the time goes in v5:
time: 356 us; the launch traced here: 354 us
  blocking collectives  140 us (39%)
  starting transfers between devices  88.9 us (25%)
  waiting for transfers between devices  65.7 us (18%)
  Pallas kernels  40.4 us (11%)
  local copies, waits for them, and re-layouts  17.7 us (5%)
    all_to_all x1, blocking collectives, exchange(): return lax.all_to_all(pieces, ALL, 0, 0, tiled=True).reshape(shape)  79.7 us
    all_to_all x3, blocking collectives, copies_to(): lax.all_to_all(jnp.broadcast_to(value, (size,) + value.shape), axis, 0, 0...  60.8 us
    ppermute x2, waiting for transfers between devices, over_op(): behind = lax.ppermute(value, 'op', [(i, (i + 3) % 4) for i in range(4)])  50.7 us
    all_to_all x2, starting transfers between devices, exchange(): return lax.all_to_all(pieces, ALL, 0, 0, tiled=True).reshape(shape)  42.8 us
    pallas_call x3, Pallas kernels, middle_stage(): pl.pallas_call(functools.partial(middle_kernel, count, sizes, turn, last)...  34.7 us
    unnamed x37, local copies, waits for them, and re-layouts  13.1 us
    ppermute x2, starting transfers between devices, over_op(): lax.ppermute(behind[half:], 'op', [(i, (i + 3) % 4) for i in range(4)])  11.4 us
    ppermute x3, starting transfers between devices, program(): lax.ppermute(own_maps, 'op', [(i, (i + k) % 4) for i in range(4)])  8.98 us
  transfers between devices with their start and end apart: 14, of which 7 were waited for; matrix products, arithmetic and copies ran while one was open for 1% of the time, Pallas kernels for 0%

profile of v5, /device:TPU:1, one launch (start us, length us, event | category | flops | bytes accessed | tf_op | source)
XLA Modules:
  0.0 354.5 jit_solution(15585528865679433579)
XLA Ops:
  1.7 29.3 %all_to_all.30 = bf16[16,2,32,128]{3,2,1,0:T(8,128)(2,1)S(1)} all-to-all(bf16[16,2,32,128]{3,2,1,0:T(8,128)(2,1)S(1)} %broadcast_in_dim.9), channel_id=1, replica_groups=mesh['op'=4,'z'=16,'y'=4,'c'=2] {'z'}, dimensions={0} | all-to-all | bytes 524288 | tf_op jit(solution)/shard_map/all_to_all | solution.py:298
  31.2 13.7 %all_to_all.31 = bf16[4,16,2,32,128]{4,3,1,2,0:T(8,128)(2,1)S(1)} all-to-all(bf16[4,16,2,32,128]{4,3,1,2,0:T(8,128)(2,1)S(1)} %broadcast_in_dim.10), channel_id=1, replica_groups=mesh['op'=4,'z'=16,'y'=4,'c'=2] {'y'}, dimensions={0} | all-to-all | bytes 2097152 | tf_op jit(solution)/shard_map/all_to_all | solution.py:298
  46.0 8.9 %collective-permute-start = (bf16[4,16,2,32,128]{4,3,1,0,2:T(8,128)(2,1)}, bf16[4,16,2,32,128]{4,3,1,0,2:T(8,128)(2,1)S(1)}, u32[]{:S(2)}, u32[]{:S(2)}) collective-permute-start(bf16[4,16,2,32,128]{4,3,1,0,2:T(8,128)(2,1)} %copy.36), channel_id=1, source_target_pairs={{0,1},{1,0},{2,3},{3,2},{4,5},{5,4},{6,7},{7,6},{8,9},{9,8},{10,11... | collective-permute-start | bytes 3145736 | tf_op jit(solution)/shard_map/ppermute | solution.py:319
  58.7 5.7 %left_stage.1 = bf16[3072,128]{1,0:T(8,128)(2,1)} custom-call(s32[8]{0:T(128)S(1)} %stack.65.info, s32[128]{0:T(128)S(1)} %bitcast.70, s32[128]{0:T(128)S(1)} %copy-done.13, s32[128]{0:T(128)S(1)} %copy-done.14, s32[128]{0:T(128)S(1)} %sub.18.row_at.col_at, bf16[64,8192]{1,0:T(8,128)(2,1)S(1)} %bitcast.67, bf16[4096,128]{1,0:T(8,128)(2,1)S(1)} %bitcast.56), custom_call_target="tpu_custom_call" | custom-call | flops 134217728 | bytes 3145728 | tf_op jit(solution)/shard_map/left_stage/pallas_call | solution.py:255
  64.4 17.7 %all-to-all-start.2 = ((bf16[512,3,2,128]{3,2,1,0:T(2,128)(2,1)}), bf16[512,3,2,128]{3,2,1,0:T(2,128)(2,1)}, u32[]{:S(2)}, u32[]{:S(2)}) async-start(bf16[512,3,2,128]{3,2,1,0:T(2,128)(2,1)} %bitcast.30), calls=%async_computation.2 | async-start | bytes 1572864 | tf_op jit(solution)/shard_map/all_to_all | solution.py:304
  82.2 4.5 %collective-permute-start.5 = (bf16[4096,128]{1,0:T(8,128)(2,1)S(1)}, bf16[4096,128]{1,0:T(8,128)(2,1)S(1)}, u32[]{:S(2)}, u32[]{:S(2)}) collective-permute-start(bf16[4096,128]{1,0:T(8,128)(2,1)S(1)} %bitcast.60), channel_id=1, source_target_pairs={{0,384},{128,0},{256,128},{384,256},{1,385},{129,1},{257,129},{385... | collective-permute-start | bytes 3145736 | tf_op jit(solution)/shard_map/ppermute | solution.py:330
  86.7 1.9 collective-permute-start.4
  88.6 25.3 %collective-permute-done.5.env_3 = bf16[4096,128]{1,0:T(8,128)(2,1)S(1)} collective-permute-done((bf16[4096,128]{1,0:T(8,128)(2,1)S(1)}, bf16[4096,128]{1,0:T(8,128)(2,1)S(1)}, u32[]{:S(2)}, u32[]{:S(2)}) %collective-permute-start.5) | collective-permute-done | bytes 1048608 | tf_op jit(solution)/shard_map/ppermute | solution.py:330
  114.7 5.7 %collective-permute-start.7 = (bf16[2048,128]{1,0:T(8,128)(2,1)}, bf16[2048,128]{1,0:T(8,128)(2,1)}, u32[]{:S(2)}, u32[]{:S(2)}) collective-permute-start(bf16[2048,128]{1,0:T(8,128)(2,1)} %slice.74), channel_id=1, source_target_pairs={{0,384},{128,0},{256,128},{384,256},{1,385},{129,1},{257,129},{385... | collective-permute-start | bytes 1572872 | tf_op jit(solution)/shard_map/ppermute | solution.py:332
  124.2 4.6 %collective-permute-start.3 = (s32[2,128]{1,0:T(2,128)S(1)}, s32[2,128]{1,0:T(2,128)S(1)}, u32[]{:S(2)}, u32[]{:S(2)}) collective-permute-start(s32[2,128]{1,0:T(2,128)S(1)} %pad_add_fusion.1), channel_id=1, source_target_pairs={{0,384},{128,0},{256,128},{384,256},{1,385},{129,1},{257,129},{385... | collective-permute-start | bytes 3080 | tf_op jit(solution)/shard_map/ppermute | solution.py:343
  130.7 2.5 collective-permute-start.1
  133.6 2.8 collective-permute-done.2
  138.0 11.8 %middle_stage.2 = bf16[3072,128]{1,0:T(8,128)(2,1)S(1)} custom-call(s32[8]{0:T(128)S(1)} %stack.65.info, s32[4,128]{1,0:T(4,128)S(1)} %get-tuple-element.16.source, s32[128]{0:T(128)S(1)} %copy-done.13, s32[128]{0:T(128)S(1)} %copy-done.14, s32[128]{0:T(128)S(1)} %sub.19.col_at, bf16[3072,128]{1,0:T(8,128)(2,1)} %bitcast.31.arrived, ...), custom_call_target="tpu_custom_call" | custom-call | flops 1073741824 | bytes 6291456 | tf_op jit(solution)/shard_map/middle_stage/pallas_call | solution.py:272
  150.7 25.2 %all-to-all-start.3 = ((bf16[512,3,2,128]{3,2,1,0:T(2,128)(2,1)}), bf16[512,3,2,128]{3,2,1,0:T(2,128)(2,1)}, u32[]{:S(2)}, u32[]{:S(2)}) async-start(bf16[512,3,2,128]{3,2,1,0:T(2,128)(2,1)} %bitcast.66), calls=%async_computation.3 | async-start | bytes 1572864 | tf_op jit(solution)/shard_map/all_to_all | solution.py:304
  175.9 4.5 %collective-permute-start.9 = (bf16[4096,128]{1,0:T(8,128)(2,1)S(1)}, bf16[4096,128]{1,0:T(8,128)(2,1)S(1)}, u32[]{:S(2)}, u32[]{:S(2)}) collective-permute-start(bf16[4096,128]{1,0:T(8,128)(2,1)S(1)} %bitcast.57), channel_id=1, source_target_pairs={{0,384},{128,0},{256,128},{384,256},{1,385},{129,1},{257,129},{385... | collective-permute-start | bytes 3145736 | tf_op jit(solution)/shard_map/ppermute | solution.py:330
  182.3 25.4 %collective-permute-done.9.env_3 = bf16[4096,128]{1,0:T(8,128)(2,1)S(1)} collective-permute-done((bf16[4096,128]{1,0:T(8,128)(2,1)S(1)}, bf16[4096,128]{1,0:T(8,128)(2,1)S(1)}, u32[]{:S(2)}, u32[]{:S(2)}) %collective-permute-start.9) | collective-permute-done | bytes 1048608 | tf_op jit(solution)/shard_map/ppermute | solution.py:330
  207.7 5.7 %collective-permute-start.11 = (bf16[2048,128]{1,0:T(8,128)(2,1)S(1)}, bf16[2048,128]{1,0:T(8,128)(2,1)S(1)}, u32[]{:S(2)}, u32[]{:S(2)}) collective-permute-start(bf16[2048,128]{1,0:T(8,128)(2,1)S(1)} %slice.76), channel_id=1, source_target_pairs={{0,384},{128,0},{256,128},{384,256},{1,385},{129,1},{257,129},{385... | collective-permute-start | bytes 1572872 | tf_op jit(solution)/shard_map/ppermute | solution.py:332
  213.5 2.1 collective-permute-start.10
  215.6 7.4 %collective-permute-done.11.env_2b = bf16[2048,128]{1,0:T(8,128)(2,1)S(1)} collective-permute-done((bf16[2048,128]{1,0:T(8,128)(2,1)S(1)}, bf16[2048,128]{1,0:T(8,128)(2,1)S(1)}, u32[]{:S(2)}, u32[]{:S(2)}) %collective-permute-start.11) | collective-permute-done | bytes 524320 | tf_op jit(solution)/shard_map/ppermute | solution.py:332
  223.8 3.8 %collective-permute-done.10.env_2a = bf16[2048,128]{1,0:T(8,128)(2,1)S(1)} collective-permute-done((bf16[2048,128]{1,0:T(8,128)(2,1)S(1)}, bf16[2048,128]{1,0:T(8,128)(2,1)S(1)}, u32[]{:S(2)}, u32[]{:S(2)}) %collective-permute-start.10) | collective-permute-done | bytes 524320 | tf_op jit(solution)/shard_map/ppermute | solution.py:331
  233.0 14.5 %middle_stage.3 = bf16[4096,128]{1,0:T(8,128)(2,1)S(1)} custom-call(s32[8]{0:T(128)S(1)} %stack.65.info, s32[4,128]{1,0:T(4,128)S(1)} %get-tuple-element.15.source, s32[128]{0:T(128)S(1)} %copy-done.14, s32[128]{0:T(128)S(1)} %copy-done.13, s32[128]{0:T(128)S(1)} %sub.18.row_at.col_at, bf16[3072,128]{1,0:T(8,128)(2,1)} %bitcast.36.arrived, ...), custom_call_target="tpu_custom_call" | custom-call | flops 1073741824 | bytes 6291456 | tf_op jit(solution)/shard_map/middle_stage/pallas_call | solution.py:272
  247.5 79.7 %all_to_all.32 = bf16[512,4,2,128]{3,2,1,0:T(2,128)(2,1)S(1)} all-to-all(bf16[512,4,2,128]{3,2,1,0:T(2,128)(2,1)S(1)} %bitcast.64), channel_id=1, replica_groups=mesh['op'=4,'z'=16,'y'=4,'c'=2] {'op','z','y','c'}, dimensions={0} | all-to-all | bytes 2097152 | tf_op jit(solution)/shard_map/all_to_all | solution.py:304
  327.2 8.4 %last_stage.1 = bf16[16,8192]{1,0:T(8,128)(2,1)S(1)} custom-call(s32[8]{0:T(128)S(1)} %stack.65.info, s32[4,128]{1,0:T(4,128)S(1)} %get-tuple-element.16.source, s32[128]{0:T(128)S(1)} %copy-done.13, s32[128]{0:T(128)S(1)} %copy-done.14, s32[128]{0:T(128)S(1)} %sub.19.col_at, bf16[4096,128]{1,0:T(8,128)(2,1)S(1)} %bitcast.65, ...), custom_call_target="tpu_custom_call" | custom-call | flops 1073741824 | bytes 6291456 | tf_op jit(solution)/shard_map/last_stage/pallas_call | solution.py:272
  335.7 17.7 %all_to_all.33 = bf16[4,16,8192]{2,1,0:T(8,128)(2,1)S(1)} all-to-all(bf16[4,16,8192]{2,1,0:T(8,128)(2,1)S(1)} %broadcast_in_dim.11), channel_id=1, replica_groups=mesh['op'=4,'z'=16,'y'=4,'c'=2] {'op'}, dimensions={0} | all-to-all | bytes 2097152 | tf_op jit(solution)/shard_map/all_to_all | solution.py:298
  (80 shorter events, 25.2 us)
Async XLA Ops:
  46.0 11.4 %collective-permute-start = (bf16[4,16,2,32,128]{4,3,1,0,2:T(8,128)(2,1)}, bf16[4,16,2,32,128]{4,3,1,0,2:T(8,128)(2,1)S(1)}, u32[]{:S(2)}, u32[]{:S(2)}) collective-permute-start(bf16[4,16,2,32,128]{4,3,1,0,2:T(8,128)(2,1)} %copy.36), channel_id=1, source_target_pairs={{0,1},{1,0},{2,3},{3,2},{4,5},{5,4},{6,7},{7,6},{8,9},{9,8},{10,11... | collective-permute-start | bytes 3145736 | tf_op jit(solution)/shard_map/ppermute | solution.py:319
  57.4 1.2 copy-start.8
  57.6 1.1 copy-start.14
  64.4 72.4 %all-to-all-start.2 = ((bf16[512,3,2,128]{3,2,1,0:T(2,128)(2,1)}), bf16[512,3,2,128]{3,2,1,0:T(2,128)(2,1)}, u32[]{:S(2)}, u32[]{:S(2)}) async-start(bf16[512,3,2,128]{3,2,1,0:T(2,128)(2,1)} %bitcast.30), calls=%async_computation.2 | async-start | bytes 1572864 | tf_op jit(solution)/shard_map/all_to_all | solution.py:304
  82.2 31.7 %collective-permute-start.5 = (bf16[4096,128]{1,0:T(8,128)(2,1)S(1)}, bf16[4096,128]{1,0:T(8,128)(2,1)S(1)}, u32[]{:S(2)}, u32[]{:S(2)}) collective-permute-start(bf16[4096,128]{1,0:T(8,128)(2,1)S(1)} %bitcast.60), channel_id=1, source_target_pairs={{0,384},{128,0},{256,128},{384,256},{1,385},{129,1},{257,129},{385... | collective-permute-start | bytes 3145736 | tf_op jit(solution)/shard_map/ppermute | solution.py:330
  86.7 33.8 %collective-permute-start.4 = (bf16[4096,128]{1,0:T(8,128)(2,1)S(1)}, bf16[4096,128]{1,0:T(8,128)(2,1)S(1)}, u32[]{:S(2)}, u32[]{:S(2)}) collective-permute-start(bf16[4096,128]{1,0:T(8,128)(2,1)S(1)} %bitcast.61), channel_id=1, source_target_pairs={{0,128},{128,256},{256,384},{384,0},{1,129},{129,257},{257,385},{3... | collective-permute-start | bytes 3145736 | tf_op jit(solution)/shard_map/ppermute | solution.py:329
  114.7 22.0 %collective-permute-start.7 = (bf16[2048,128]{1,0:T(8,128)(2,1)}, bf16[2048,128]{1,0:T(8,128)(2,1)}, u32[]{:S(2)}, u32[]{:S(2)}) collective-permute-start(bf16[2048,128]{1,0:T(8,128)(2,1)} %slice.74), channel_id=1, source_target_pairs={{0,384},{128,0},{256,128},{384,256},{1,385},{129,1},{257,129},{385... | collective-permute-start | bytes 1572872 | tf_op jit(solution)/shard_map/ppermute | solution.py:332
  122.3 14.5 %collective-permute-start.6 = (bf16[2048,128]{1,0:T(8,128)(2,1)}, bf16[2048,128]{1,0:T(8,128)(2,1)}, u32[]{:S(2)}, u32[]{:S(2)}) collective-permute-start(bf16[2048,128]{1,0:T(8,128)(2,1)} %slice.73), channel_id=1, source_target_pairs={{0,128},{128,256},{256,384},{384,0},{1,129},{129,257},{257,385},{3... | collective-permute-start | bytes 1572872 | tf_op jit(solution)/shard_map/ppermute | solution.py:331
  124.2 9.4 %collective-permute-start.3 = (s32[2,128]{1,0:T(2,128)S(1)}, s32[2,128]{1,0:T(2,128)S(1)}, u32[]{:S(2)}, u32[]{:S(2)}) collective-permute-start(s32[2,128]{1,0:T(2,128)S(1)} %pad_add_fusion.1), channel_id=1, source_target_pairs={{0,384},{128,0},{256,128},{384,256},{1,385},{129,1},{257,129},{385... | collective-permute-start | bytes 3080 | tf_op jit(solution)/shard_map/ppermute | solution.py:343
  128.8 7.7 %collective-permute-start.2 = (s32[2,128]{1,0:T(2,128)S(1)}, s32[2,128]{1,0:T(2,128)S(1)}, u32[]{:S(2)}, u32[]{:S(2)}) collective-permute-start(s32[2,128]{1,0:T(2,128)S(1)} %pad_add_fusion.1), channel_id=1, source_target_pairs={{0,256},{128,384},{256,0},{384,128},{1,257},{129,385},{257,1},{385... | collective-permute-start | bytes 3080 | tf_op jit(solution)/shard_map/ppermute | solution.py:343
  130.7 6.0 %collective-permute-start.1 = (s32[2,128]{1,0:T(2,128)S(1)}, s32[2,128]{1,0:T(2,128)S(1)}, u32[]{:S(2)}, u32[]{:S(2)}) collective-permute-start(s32[2,128]{1,0:T(2,128)S(1)} %pad_add_fusion.1), channel_id=1, source_target_pairs={{0,128},{128,256},{256,384},{384,0},{1,129},{129,257},{257,385},{3... | collective-permute-start | bytes 3080 | tf_op jit(solution)/shard_map/ppermute | solution.py:343
  136.8 1.2 copy-start.1
  150.7 77.7 %all-to-all-start.3 = ((bf16[512,3,2,128]{3,2,1,0:T(2,128)(2,1)}), bf16[512,3,2,128]{3,2,1,0:T(2,128)(2,1)}, u32[]{:S(2)}, u32[]{:S(2)}) async-start(bf16[512,3,2,128]{3,2,1,0:T(2,128)(2,1)} %bitcast.66), calls=%async_computation.3 | async-start | bytes 1572864 | tf_op jit(solution)/shard_map/all_to_all | solution.py:304
  175.9 31.8 %collective-permute-start.9 = (bf16[4096,128]{1,0:T(8,128)(2,1)S(1)}, bf16[4096,128]{1,0:T(8,128)(2,1)S(1)}, u32[]{:S(2)}, u32[]{:S(2)}) collective-permute-start(bf16[4096,128]{1,0:T(8,128)(2,1)S(1)} %bitcast.57), channel_id=1, source_target_pairs={{0,384},{128,0},{256,128},{384,256},{1,385},{129,1},{257,129},{385... | collective-permute-start | bytes 3145736 | tf_op jit(solution)/shard_map/ppermute | solution.py:330
  180.4 33.1 %collective-permute-start.8 = (bf16[4096,128]{1,0:T(8,128)(2,1)S(1)}, bf16[4096,128]{1,0:T(8,128)(2,1)S(1)}, u32[]{:S(2)}, u32[]{:S(2)}) collective-permute-start(bf16[4096,128]{1,0:T(8,128)(2,1)S(1)} %bitcast.58), channel_id=1, source_target_pairs={{0,128},{128,256},{256,384},{384,0},{1,129},{129,257},{257,385},{3... | collective-permute-start | bytes 3145736 | tf_op jit(solution)/shard_map/ppermute | solution.py:329
  207.7 5.8 %copy-start.4 = (bf16[4096,128]{1,0:T(8,128)(2,1)}, bf16[4096,128]{1,0:T(8,128)(2,1)S(1)}, u32[]{:S(2)}) copy-start(bf16[4096,128]{1,0:T(8,128)(2,1)S(1)} %collective-permute-done.9.env_3) | copy-start | bytes 3145732
  207.7 15.3 %collective-permute-start.11 = (bf16[2048,128]{1,0:T(8,128)(2,1)S(1)}, bf16[2048,128]{1,0:T(8,128)(2,1)S(1)}, u32[]{:S(2)}, u32[]{:S(2)}) collective-permute-start(bf16[2048,128]{1,0:T(8,128)(2,1)S(1)} %slice.76), channel_id=1, source_target_pairs={{0,384},{128,0},{256,128},{384,256},{1,385},{129,1},{257,129},{385... | collective-permute-start | bytes 1572872 | tf_op jit(solution)/shard_map/ppermute | solution.py:332
  213.4 2.2 copy-start.6
  213.5 14.1 %collective-permute-start.10 = (bf16[2048,128]{1,0:T(8,128)(2,1)S(1)}, bf16[2048,128]{1,0:T(8,128)(2,1)S(1)}, u32[]{:S(2)}, u32[]{:S(2)}) collective-permute-start(bf16[2048,128]{1,0:T(8,128)(2,1)S(1)} %slice.75), channel_id=1, source_target_pairs={{0,128},{128,256},{256,384},{384,0},{1,129},{129,257},{257,385},{3... | collective-permute-start | bytes 1572872 | tf_op jit(solution)/shard_map/ppermute | solution.py:331
  228.4 1.2 copy-start.5
  229.7 1.2 copy-start.7
  230.9 1.0 copy-start.10
  231.9 1.0 copy-start.12
  247.5 79.7 %copy-start.2 = (bf16[4096,128]{1,0:T(8,128)(2,1)S(1)}, bf16[4096,128]{1,0:T(8,128)(2,1)}, u32[]{:S(2)}) copy-start(bf16[4096,128]{1,0:T(8,128)(2,1)} %copy-done) | copy-start | bytes 3145732
  (8 other events, 6.2 us)
